TPU v7x, 32 devices: a whole 2x2x4 slice. The times are simulated.
32 devices in a mesh: space: 8 (over z, y), halo: 4 (over x, core).
Axes of the slice: x: 2, y: 2, z: 4, core: 2. Of those that a mesh axis runs over, the one named last changes fastest.
Arguments:
- positions: float32 [3, 131072], P(None, 'space'), may hold values from -1 to 1
- masses: float32 [131072], P('space'), may hold values from 0.1 to 10
- centres: float32 [4, 3, 128], P('halo'), may hold values from -0.5 to 0.5
- pair_halo: int32 [4, 2048], P('halo', 'space'), may hold values from 0 to 127
- pair_tile: int32 [4, 2048], P('halo', 'space'), may hold values from 0 to 31
- halo_slot: int32 [4, 128], P('halo'), may hold values from 0 to 127, each once within a row
- feedback: float32 [4, 128], P('halo', 'space'), may hold values from 0.5 to 1.5
- mixing: float32 [3, 128, 128], replicated, may hold values from -0.5 to 0.5
- drive: float32 [3, 128], replicated, may hold values from 0.2 to 1
- readout: float32 [3, 128], replicated, may hold values from -1.5 to 1.5
Outputs:
- displacement: float32 [3, 131072], P(None, 'space')
All inputs are finite; a program needn't handle non-finite values.
Results may differ from a plain program's by a relative error of at most 0.0003.
Values sent between devices are 32-bit elements; how exact they have to be, the bound alone decides.
No kernel may reach another device: no remote copies, remote signals or barrier semaphores. Data moves between devices by JAX's collectives and lax.ppermute only.
A program may use at most 64 MiB of HBM per device.

v0:
```python
import jax
import jax.numpy as jnp
from jax import lax
from jax.sharding import PartitionSpec as P

BLK = 512
ITERS = 8


def spline_basis(offset, knots):
    radial_distance = jnp.sqrt(jnp.sum(offset * offset, axis=0))
    scaled = radial_distance * ((knots - 1) / 2.6)
    knot_index = jnp.arange(knots, dtype=jnp.float32)
    return jnp.maximum(0.0, 1.0 - jnp.abs(scaled[..., None] - knot_index))


def relax(level, phi, mixing, drive, readout):
    state = jnp.zeros((3,) + level.shape, jnp.float32)
    for relax_iteration in range(ITERS):
        average = jnp.mean(state, axis=0)
        fresh = []
        for comp in range(3):
            mixed = jnp.dot(state[comp], mixing[comp], precision=lax.Precision.HIGHEST)
            fresh.append(jnp.tanh(drive[comp] * level + phi[:, None] * mixed + 0.5 * average))
        state = jnp.stack(fresh)
    return jnp.sum(state * readout[:, None, :], axis=0)


def per_device(
    positions, masses, centres, pair_halo, pair_tile, halo_slot, feedback, mixing, drive, readout
):
    knots = mixing.shape[1]
    tile_count = masses.shape[0] // BLK
    number_of_pairs = pair_halo.shape[1]
    places = positions.reshape(3, tile_count, BLK)
    weights = masses.reshape(tile_count, BLK)
    halo_ids = pair_halo[0]
    tile_ids = pair_tile[0]
    centre_rows = centres[0]
    slot_ids = halo_slot[0][halo_ids]
    block = min(64, number_of_pairs // 8)
    offsets = places[:, tile_ids, :] - centre_rows[:, halo_ids][:, :, None]
    offset_blocks = jnp.transpose(offsets.reshape(3, -1, block, BLK), (1, 0, 2, 3))
    weight_blocks = weights[tile_ids].reshape(-1, block, BLK)

    def project(inputs):
        offset_part, weight_part = inputs
        basis = spline_basis(offset_part, knots)
        return jnp.sum(weight_part[:, :, None] * basis, axis=1)

    pair_rows = lax.map(project, (offset_blocks, weight_blocks)).reshape(number_of_pairs, knots)
    slot_total = halo_slot.shape[1]
    wanted = jnp.arange(slot_total, dtype=jnp.int32)
    halo_selection = (slot_ids[None, :] == wanted[:, None]).astype(jnp.float32)
    dense = lax.psum(jnp.dot(halo_selection, pair_rows, precision=lax.Precision.HIGHEST), "space")
    all_feedback = lax.all_gather(feedback[0], "space", axis=0, tiled=True)
    coef_table = relax(jnp.log1p(dense), all_feedback, mixing, drive, readout)
    coef_rows = coef_table[slot_ids].reshape(-1, block, knots)

    def evaluate(inputs):
        offset_part, coef_part = inputs
        basis = spline_basis(offset_part, knots)
        scalar = jnp.sum(basis * coef_part[:, None, :], axis=2)
        return offset_part * scalar[None]

    shifted_positions = lax.map(evaluate, (offset_blocks, coef_rows))
    shifted_positions = jnp.transpose(shifted_positions, (1, 0, 2, 3)).reshape(
        3, number_of_pairs, BLK
    )
    current_tile = jnp.arange(tile_count, dtype=jnp.int32)
    halo_selection = (current_tile[:, None] == tile_ids[None, :]).astype(jnp.float32)
    partial_halo_sum = jnp.einsum(
        "dq,vqn->vdn", halo_selection, shifted_positions, precision=lax.Precision.HIGHEST
    )
    partial_halo_sum = partial_halo_sum.reshape(3, tile_count * BLK)
    return lax.psum(partial_halo_sum, "halo")


def solution(mesh):
    return jax.shard_map(
        per_device,
        mesh=mesh,
        in_specs=(
            P(None, "space"),
            P("space"),
            P("halo", None, None),
            P("halo", "space"),
            P("halo", "space"),
            P("halo", None),
            P("halo", "space"),
            P(),
            P(),
            P(),
        ),
        out_specs=P(None, "space"),
        check_vma=False,
    )
```

profile of v0, /device:TPU:0, one launch (start us, length us, event | category | flops | bytes accessed | tf_op | source)
XLA Modules:
  0.0 229.1 jit_solution(4436138836586837490)
XLA Ops:
  7.5 1.9 gather_fusion
  15.5 40.7 %while.20 = (s32[]{:T(128)}, f32[8,32,128]{2,1,0:T(8,128)S(1)}, f32[8,32,512]{2,1,0:T(8,128)S(1)}, f32[8,3,32,512]{3,2,1,0:T(8,128)S(1)}, s32[]{:T(128)}) while((s32[]{:T(128)}, f32[8,32,128]{2,1,0:T(8,128)S(1)}, f32[8,32,512]{2,1,0:T(8,128)S(1)}, f32[8,3,32,512]{3,2,1,0:T(8,128)S(1)}, s32[]{:T(128)}) %tuple.50), condition=%wide.region_3.4_spmd, body=%wide.region_0.3_spmd.sunk | while | flops 12677122 | bytes 704585 | solution.py:51
  15.6 5.0 %multiply_reduce_fusion.9 = f32[32,128]{1,0:T(8,128)S(1)} fusion(f32[32,512]{1,0:T(8,128)S(1)} %sqrt_multiply_fusion.4, f32[32,512]{1,0:T(8,128)S(1)} %dynamic-slice_bitcast_fusion.4), kind=kLoop, calls=%fused_computation.5.clone.1 | loop fusion | flops 12578816 | bytes 147456 | tf_op jit(solution)/shard_map/while/body/eval_jaxpr/reduce_sum | solution.py:49
  20.7 5.0 %multiply_reduce_fusion.9 = f32[32,128]{1,0:T(8,128)S(1)} fusion(f32[32,512]{1,0:T(8,128)S(1)} %sqrt_multiply_fusion.4, f32[32,512]{1,0:T(8,128)S(1)} %dynamic-slice_bitcast_fusion.4), kind=kLoop, calls=%fused_computation.5.clone.1 | loop fusion | flops 12578816 | bytes 147456 | tf_op jit(solution)/shard_map/while/body/eval_jaxpr/reduce_sum | solution.py:49
  25.8 5.0 %multiply_reduce_fusion.9 = f32[32,128]{1,0:T(8,128)S(1)} fusion(f32[32,512]{1,0:T(8,128)S(1)} %sqrt_multiply_fusion.4, f32[32,512]{1,0:T(8,128)S(1)} %dynamic-slice_bitcast_fusion.4), kind=kLoop, calls=%fused_computation.5.clone.1 | loop fusion | flops 12578816 | bytes 147456 | tf_op jit(solution)/shard_map/while/body/eval_jaxpr/reduce_sum | solution.py:49
  30.9 5.0 %multiply_reduce_fusion.9 = f32[32,128]{1,0:T(8,128)S(1)} fusion(f32[32,512]{1,0:T(8,128)S(1)} %sqrt_multiply_fusion.4, f32[32,512]{1,0:T(8,128)S(1)} %dynamic-slice_bitcast_fusion.4), kind=kLoop, calls=%fused_computation.5.clone.1 | loop fusion | flops 12578816 | bytes 147456 | tf_op jit(solution)/shard_map/while/body/eval_jaxpr/reduce_sum | solution.py:49
  35.9 5.0 %multiply_reduce_fusion.9 = f32[32,128]{1,0:T(8,128)S(1)} fusion(f32[32,512]{1,0:T(8,128)S(1)} %sqrt_multiply_fusion.4, f32[32,512]{1,0:T(8,128)S(1)} %dynamic-slice_bitcast_fusion.4), kind=kLoop, calls=%fused_computation.5.clone.1 | loop fusion | flops 12578816 | bytes 147456 | tf_op jit(solution)/shard_map/while/body/eval_jaxpr/reduce_sum | solution.py:49
  41.0 5.0 %multiply_reduce_fusion.9 = f32[32,128]{1,0:T(8,128)S(1)} fusion(f32[32,512]{1,0:T(8,128)S(1)} %sqrt_multiply_fusion.4, f32[32,512]{1,0:T(8,128)S(1)} %dynamic-slice_bitcast_fusion.4), kind=kLoop, calls=%fused_computation.5.clone.1 | loop fusion | flops 12578816 | bytes 147456 | tf_op jit(solution)/shard_map/while/body/eval_jaxpr/reduce_sum | solution.py:49
  46.1 5.0 %multiply_reduce_fusion.9 = f32[32,128]{1,0:T(8,128)S(1)} fusion(f32[32,512]{1,0:T(8,128)S(1)} %sqrt_multiply_fusion.4, f32[32,512]{1,0:T(8,128)S(1)} %dynamic-slice_bitcast_fusion.4), kind=kLoop, calls=%fused_computation.5.clone.1 | loop fusion | flops 12578816 | bytes 147456 | tf_op jit(solution)/shard_map/while/body/eval_jaxpr/reduce_sum | solution.py:49
  51.2 5.0 %multiply_reduce_fusion.9 = f32[32,128]{1,0:T(8,128)S(1)} fusion(f32[32,512]{1,0:T(8,128)S(1)} %sqrt_multiply_fusion.4, f32[32,512]{1,0:T(8,128)S(1)} %dynamic-slice_bitcast_fusion.4), kind=kLoop, calls=%fused_computation.5.clone.1 | loop fusion | flops 12578816 | bytes 147456 | tf_op jit(solution)/shard_map/while/body/eval_jaxpr/reduce_sum | solution.py:49
  56.2 1.9 gather_fusion.2
  60.6 23.2 %all-reduce = f32[128]{0:T(128)S(1)} all-reduce(f32[128]{0:T(128)S(1)} %bitcast_dynamic-update-slice_fusion.2), channel_id=2, replica_groups=mesh['space'=8,'halo'=4] {'space'}, use_global_device_ids=true, to_apply=%add | all-reduce | flops 128 | bytes 1024
  83.8 47.3 %all-reduce.4.cloned.1.call-done = f32[128,128]{1,0:T(8,128)} async-done(((f32[128,128]{1,0:T(8,128)}), f32[128,128]{1,0:T(8,128)}) %all-reduce.4.cloned.1.call-update) | async-done | bytes 65552 | tf_op jit(solution)/shard_map/psum | solution.py:55
  141.2 44.0 %while.21 = (s32[]{:T(128)}, f32[8,3,32,512]{3,2,0,1:T(8,128)}, f32[8,3,32,512]{3,2,1,0:T(8,128)S(1)}, f32[8,32,128]{2,1,0:T(8,128)S(1)}, s32[]{:T(128)}) while((s32[]{:T(128)}, f32[8,3,32,512]{3,2,0,1:T(8,128)}, f32[8,3,32,512]{3,2,1,0:T(8,128)S(1)}, f32[8,32,128]{2,1,0:T(8,128)S(1)}, s32[]{:T(128)}) %tuple.51), condition=%wide.region_12.13_spmd, body=%wide.region_9.12_spmd.sunk | while | flops 12713986 | bytes 1032773 | solution.py:66
  141.3 4.7 %multiply_reduce_fusion.11 = f32[32,512]{1,0:T(8,128)S(1)} fusion(f32[32,128]{1,0:T(8,128)S(1)} %dynamic-slice_bitcast_fusion.5, f32[32,512]{1,0:T(8,128)S(1)} %sqrt_multiply_fusion.5), kind=kLoop, calls=%fused_computation.10.clone.1 | loop fusion | flops 12566528 | bytes 147456 | tf_op jit(solution)/shard_map/while/body/eval_jaxpr/reduce_sum | solution.py:63
  146.8 4.7 %multiply_reduce_fusion.11 = f32[32,512]{1,0:T(8,128)S(1)} fusion(f32[32,128]{1,0:T(8,128)S(1)} %dynamic-slice_bitcast_fusion.5, f32[32,512]{1,0:T(8,128)S(1)} %sqrt_multiply_fusion.5), kind=kLoop, calls=%fused_computation.10.clone.1 | loop fusion | flops 12566528 | bytes 147456 | tf_op jit(solution)/shard_map/while/body/eval_jaxpr/reduce_sum | solution.py:63
  152.3 4.7 %multiply_reduce_fusion.11 = f32[32,512]{1,0:T(8,128)S(1)} fusion(f32[32,128]{1,0:T(8,128)S(1)} %dynamic-slice_bitcast_fusion.5, f32[32,512]{1,0:T(8,128)S(1)} %sqrt_multiply_fusion.5), kind=kLoop, calls=%fused_computation.10.clone.1 | loop fusion | flops 12566528 | bytes 147456 | tf_op jit(solution)/shard_map/while/body/eval_jaxpr/reduce_sum | solution.py:63
  157.8 4.7 %multiply_reduce_fusion.11 = f32[32,512]{1,0:T(8,128)S(1)} fusion(f32[32,128]{1,0:T(8,128)S(1)} %dynamic-slice_bitcast_fusion.5, f32[32,512]{1,0:T(8,128)S(1)} %sqrt_multiply_fusion.5), kind=kLoop, calls=%fused_computation.10.clone.1 | loop fusion | flops 12566528 | bytes 147456 | tf_op jit(solution)/shard_map/while/body/eval_jaxpr/reduce_sum | solution.py:63
  163.3 4.7 %multiply_reduce_fusion.11 = f32[32,512]{1,0:T(8,128)S(1)} fusion(f32[32,128]{1,0:T(8,128)S(1)} %dynamic-slice_bitcast_fusion.5, f32[32,512]{1,0:T(8,128)S(1)} %sqrt_multiply_fusion.5), kind=kLoop, calls=%fused_computation.10.clone.1 | loop fusion | flops 12566528 | bytes 147456 | tf_op jit(solution)/shard_map/while/body/eval_jaxpr/reduce_sum | solution.py:63
  168.8 4.7 %multiply_reduce_fusion.11 = f32[32,512]{1,0:T(8,128)S(1)} fusion(f32[32,128]{1,0:T(8,128)S(1)} %dynamic-slice_bitcast_fusion.5, f32[32,512]{1,0:T(8,128)S(1)} %sqrt_multiply_fusion.5), kind=kLoop, calls=%fused_computation.10.clone.1 | loop fusion | flops 12566528 | bytes 147456 | tf_op jit(solution)/shard_map/while/body/eval_jaxpr/reduce_sum | solution.py:63
  174.3 4.7 %multiply_reduce_fusion.11 = f32[32,512]{1,0:T(8,128)S(1)} fusion(f32[32,128]{1,0:T(8,128)S(1)} %dynamic-slice_bitcast_fusion.5, f32[32,512]{1,0:T(8,128)S(1)} %sqrt_multiply_fusion.5), kind=kLoop, calls=%fused_computation.10.clone.1 | loop fusion | flops 12566528 | bytes 147456 | tf_op jit(solution)/shard_map/while/body/eval_jaxpr/reduce_sum | solution.py:63
  179.8 4.7 %multiply_reduce_fusion.11 = f32[32,512]{1,0:T(8,128)S(1)} fusion(f32[32,128]{1,0:T(8,128)S(1)} %dynamic-slice_bitcast_fusion.5, f32[32,512]{1,0:T(8,128)S(1)} %sqrt_multiply_fusion.5), kind=kLoop, calls=%fused_computation.10.clone.1 | loop fusion | flops 12566528 | bytes 147456 | tf_op jit(solution)/shard_map/while/body/eval_jaxpr/reduce_sum | solution.py:63
  185.2 2.1 convolution_bitcast_fusion
  188.2 32.4 %all-reduce.6.cloned.1.call-done = f32[3,16384]{1,0:T(4,128)} async-done(((f32[3,16384]{1,0:T(4,128)}), f32[3,16384]{1,0:T(4,128)}) %all-reduce.6.cloned.1.call-update) | async-done | bytes 196624 | tf_op jit(solution)/shard_map/psum | solution.py:76
  (139 shorter events, 27.8 us)
Async XLA Ops:
  6.5 1.0 copy-start
  6.5 124.6 %all-reduce.4.cloned.1.call-start = ((), (), s32[]{:S(2)}) async-start(), calls=%async_computation | async-start | bytes 131072 | tf_op jit(solution)/shard_map/psum | solution.py:55
  9.4 1.7 copy-start.9
  9.4 1.7 copy-start.7
  13.6 0.8 copy-start.4
  15.4 40.8 %copy-start.1 = (s32[1,128]{1,0:T(1,128)S(1)}, s32[1,128]{1,0:T(1,128)}, u32[]{:S(2)}) copy-start(s32[1,128]{1,0:T(1,128)} %param.19) | copy-start | bytes 1540
  15.4 43.6 %copy-start.11 = (u32[32]{0:T(128)S(1)}, u32[32]{0:T(128)}, u32[]{:S(2)}) copy-start(u32[32]{0:T(128)} %constant.81) | copy-start | bytes 388
  15.4 45.0 %copy-start.10 = (f32[1,16]{1,0:T(1,128)S(1)}, f32[1,16]{1,0:T(1,128)}, u32[]{:S(2)}) copy-start(f32[1,16]{1,0:T(1,128)} %param.20) | copy-start | bytes 196
  15.5 68.2 %copy-start.8 = (f32[3,128]{1,0:T(4,128)S(1)}, f32[3,128]{1,0:T(4,128)}, u32[]{:S(2)}) copy-start(f32[3,128]{1,0:T(4,128)} %param.22) | copy-start | bytes 4612
  15.5 68.2 %copy-start.3 = (f32[3,128,128]{2,1,0:T(8,128)S(1)}, f32[3,128,128]{2,1,0:T(8,128)}, u32[]{:S(2)}) copy-start(f32[3,128,128]{2,1,0:T(8,128)} %param.21) | copy-start | bytes 589828
  59.0 161.6 %all-reduce.6.cloned.1.call-start = ((), (), s32[]{:S(2)}) async-start(), calls=%async_computation.1 | async-start | bytes 524288 | tf_op jit(solution)/shard_map/psum | solution.py:76
  131.1 5.7 %copy-start.2 = (f32[128,128]{1,0:T(8,128)S(1)}, f32[128,128]{1,0:T(8,128)}, u32[]{:S(2)}) copy-start(f32[128,128]{1,0:T(8,128)} %all-reduce.4.cloned.1.call-done) | copy-start | bytes 196612
  138.0 2.5 %copy-start.6 = (f32[3,128]{1,0:T(4,128)S(1)}, f32[3,128]{1,0:T(4,128)}, u32[]{:S(2)}) copy-start(f32[3,128]{1,0:T(4,128)} %param.23) | copy-start | bytes 4612
  141.2 44.0 %copy-start.5 = (s32[1,256]{1,0:T(1,128)S(1)}, s32[1,256]{1,0:T(1,128)}, u32[]{:S(2)}) copy-start(s32[1,256]{1,0:T(1,128)} %param.18) | copy-start | bytes 3076
Sparse Core Ops, SparseCore 0:
  59.1 71.9 all-reduce.3
  188.3 32.2 all-reduce.5
where the time goes:
time: 230 us; the launch traced here: 229 us
  other arithmetic  86.2 us (37%)
  waiting for transfers between devices  79.7 us (35%)
  blocking collectives  23.2 us (10%)
  between operations  14.5 us (6%)
  local copies, waits for them, and re-layouts  12.7 us (6%)
  matrix products  12.1 us (5%)
    psum x1, waiting for transfers between devices, per_device(): lax.psum(jnp.dot(halo_selection, pair_rows, precision=lax.Precision.HIGHE...  47.3 us
    reduce_sum x8, other arithmetic, project(): return jnp.sum(weight_part[:, :, None] * basis, axis=1)  39.8 us
    reduce_sum x8, other arithmetic, evaluate(): scalar = jnp.sum(basis * coef_part[:, None, :], axis=2)  37.7 us
    psum x1, waiting for transfers between devices, per_device(): return lax.psum(partial_halo_sum, 'halo')  32.4 us
    unnamed x1, blocking collectives  23.2 us
    dot_general x21, matrix products, relax(): mixed = jnp.dot(state[comp], mixing[comp], precision=lax.Precision.HIGHEST)  9.13 us
    dynamic_update_slice x8, other arithmetic, per_device(): shifted_positions = lax.map(evaluate, (offset_blocks, coef_rows))  5.63 us
  transfers between devices with their start and end apart: 2, of which 2 were waited for; matrix products, arithmetic and copies ran while one was open for 0% of the time, Pallas kernels for 0%

commit v1 on v0

v1 whole, which is shorter than its diff:
```python
import functools

import jax
import jax.numpy as jnp
from jax import lax
from jax.experimental import pallas as pl
from jax.experimental.pallas import tpu as pltpu
from jax.sharding import PartitionSpec as P

BLK = 512
ITERS = 8
LANES = 128
ROWS = 16
F32, BF16 = jnp.float32, jnp.bfloat16


def iota(shape, axis):
    return lax.broadcasted_iota(jnp.int32, shape, axis)


def parts_of(value, count):
    parts = []
    for at in range(count):
        parts.append(value.astype(BF16))
        if at + 1 < count:
            value = value - parts[-1].astype(F32)
    return parts


def bdot(a, b):
    return lax.dot_general(a, b, (((1,), (0,)), ((), ())), preferred_element_type=F32)


def bdot_t(a, b):
    return lax.dot_general(a, b, (((1,), (1,)), ((), ())), preferred_element_type=F32)


def lane_gather(table, index):
    return jnp.take_along_axis(table, index, axis=1, mode="promise_in_bounds")


def pair_centres(cen_ref, halo_row):
    pairs, halos = halo_row.shape[1], cen_ref.shape[2]
    cen = jnp.concatenate([cen_ref[0], jnp.zeros((5, halos), F32)], axis=0)
    blocks = []
    for at in range(pairs // LANES):
        ids = jnp.broadcast_to(halo_row[:, at * LANES : (at + 1) * LANES], (8, LANES))
        found = jnp.zeros((8, LANES), F32)
        for block in range(halos // LANES):
            here = lane_gather(cen[:, block * LANES : (block + 1) * LANES], ids % LANES)
            found = jnp.where(ids // LANES == block, here, found)
        blocks.append(found)
    return jnp.concatenate(blocks, axis=1)


def project_kernel(
    pos_ref, mass_ref, cen_ref, halo_ref, tile_ref, slot_ref, feed_ref,
    out_ref, u_ref, pos_out_ref, m_ref, spread_ref,
):
    pairs, halos = halo_ref.shape[1], slot_ref.shape[1]
    tiles = pos_out_ref.shape[1]
    knots = out_ref.shape[1]
    chunks = BLK // LANES
    for tile in range(tiles):
        block = pos_ref[:, tile * BLK : (tile + 1) * BLK]
        for axis in range(3):
            pos_out_ref[axis, tile : tile + 1, :] = block[axis : axis + 1, :]
    mass = jnp.concatenate(
        [mass_ref[pl.ds(at, tiles, stride=chunks), :] for at in range(chunks)], axis=1
    )
    table = [pos_out_ref[0], pos_out_ref[1], pos_out_ref[2], mass]
    table = jnp.concatenate(
        [jnp.concatenate(three, axis=0) for three in zip(*[parts_of(t, 3) for t in table])]
        if False
        else [jnp.concatenate(parts_of(t, 3), axis=0) for t in table],
        axis=1,
    )
    centre = pair_centres(cen_ref, halo_ref[...])
    row = iota((8, pairs), 0)
    columns = jnp.where(row == 3, jnp.broadcast_to(tile_ref[...], (8, pairs)).astype(F32), centre)
    columns = jnp.transpose(columns)
    tile_of = columns[:, 3:4].astype(jnp.int32)
    lane = iota((pairs, 3 * tiles), 1)
    select = jnp.where(lane % tiles == tile_of, 1.0, 0.0).astype(BF16)
    found = bdot(select, table)
    square = jnp.zeros((pairs, BLK), F32)
    for axis in range(3):
        offset = found[:, axis * BLK : (axis + 1) * BLK] - columns[:, axis : axis + 1]
        square = square + offset * offset
    u_ref[...] = jnp.sqrt(square) * ((knots - 1) / 2.6)
    m_ref[...] = found[:, 3 * BLK :]

    highs = knots // ROWS
    lane = iota((ROWS, LANES), 1)
    sub = iota((ROWS, LANES), 0)
    index = (lane % 8) * ROWS + sub

    def group(at, carry):
        rows = pl.ds(pl.multiple_of(at * ROWS, ROWS), ROWS)
        u = u_ref[rows, :]
        m = m_ref[rows, :]
        whole = jnp.floor(u)
        after = m * (u - whole)
        high = jnp.floor(whole * (1.0 / ROWS))
        low = (whole - high * ROWS).astype(BF16)
        high = high.astype(BF16)
        zero = jnp.zeros(u.shape, BF16)
        one = jnp.ones(u.shape, BF16)
        values = parts_of(m - after, 2) + parts_of(after, 2)
        left = jnp.concatenate(
            [jnp.where(high == h, v, zero) for v in values for h in range(highs)], axis=0
        )
        right = jnp.concatenate([jnp.where(low == b, one, zero) for b in range(ROWS)], axis=0)
        both = bdot_t(left, right)
        for which in range(2):
            spread = jnp.zeros((ROWS, knots), F32)
            for h in range(highs):
                first = ((2 * which) * highs + h) * ROWS
                second = ((2 * which + 1) * highs + h) * ROWS
                tile = both[first : first + ROWS] + both[second : second + ROWS]
                for half in range(2):
                    here = lane_gather(tile[:, half * LANES : (half + 1) * LANES], index)
                    spread = jnp.where(lane // 8 == 2 * h + half, here, spread)
            spread_ref[rows, which * knots : (which + 1) * knots] = spread
        return carry

    lax.fori_loop(0, pairs // ROWS, group, 0)

    owner = jnp.broadcast_to(halo_ref[...], (halos, pairs)) == iota((halos, pairs), 0)
    owner = jnp.where(owner, 1.0, 0.0).astype(BF16)
    total = sum(bdot(owner, part) for part in parts_of(spread_ref[...], 3))
    out_ref[:halos, :] = total[:, :knots] + pltpu.roll(total[:, knots:], 1, 1)

    mine = feed_ref.shape[1]
    slot = slot_ref[...] - lax.axis_index("space") * mine
    phi = jnp.zeros((1, halos), F32)
    for at in range(mine):
        phi = jnp.where(slot == at, feed_ref[0, at], phi)
    out_ref[halos:, :] = jnp.zeros((out_ref.shape[0] - halos, knots), F32)
    for at in range(halos // LANES):
        out_ref[halos + at : halos + at + 1, :] = phi[:, at * LANES : (at + 1) * LANES]


def relax_kernel(
    count, halo_axis, *refs,
):
    profile_refs = refs[:count]
    (
        u_ref, pos_ref, cen_ref, halo_ref, tile_ref, mix_ref, drive_ref, readout_ref,
        keep_ref, send_ref, state_ref, base_ref, weight_ref, table_ref, out_ref,
    ) = refs[count:]
    pairs, halos = halo_ref.shape[1], cen_ref.shape[2]
    tiles, knots = pos_ref.shape[1], drive_ref.shape[1]
    for comp in range(3):
        high, low = parts_of(mix_ref[comp], 2)
        both = jnp.concatenate([high, low], axis=1)
        weight_ref[comp] = jnp.concatenate([both, both], axis=0)
    extra = sum(ref[halos:, :] for ref in profile_refs)
    phi_columns = jnp.transpose(extra)
    for block in range(halos // LANES):
        rows = slice(block * LANES, (block + 1) * LANES)
        level = jnp.log1p(sum(ref[rows, :] for ref in profile_refs))
        phi = phi_columns[:, block : block + 1]
        for comp in range(3):
            base = drive_ref[comp : comp + 1, :] * level
            base_ref[comp] = base
            state_ref[comp] = jnp.tanh(base)

        def step(at, carry):
            old = [state_ref[comp] for comp in range(3)]
            half_mean = (old[0] + old[1] + old[2]) * (0.5 / 3.0)
            for comp in range(3):
                split = jnp.concatenate(parts_of(old[comp], 2), axis=1)
                mixed = bdot(split, weight_ref[comp])
                mixed = mixed[:, :knots] + mixed[:, knots:]
                state_ref[comp] = jnp.tanh(base_ref[comp] + phi * mixed + half_mean)
            return carry

        lax.fori_loop(0, ITERS - 1, step, 0)
        coef = sum(state_ref[comp] * readout_ref[comp : comp + 1, :] for comp in range(3))
        table_ref[rows, :knots] = coef
        table_ref[rows, knots:] = pltpu.roll(coef, knots - 1, 1) - coef

    halo_row, tile_row = halo_ref[...], tile_ref[...]
    halo_column = jnp.transpose(jnp.broadcast_to(halo_row, (8, pairs)).astype(F32))[:, :1]
    owner = jnp.where(halo_column.astype(jnp.int32) == iota((pairs, halos), 1), 1.0, 0.0).astype(BF16)
    tables = sum(bdot(owner, part) for part in parts_of(table_ref[...], 3))
    scalars = []
    for at in range(BLK // LANES):
        u = u_ref[:, at * LANES : (at + 1) * LANES]
        whole = jnp.floor(u)
        index = whole.astype(jnp.int32)
        start = lane_gather(tables[:, :knots], index)
        slope = lane_gather(tables[:, knots:], index)
        scalars.append(start + (u - whole) * slope)
    high, low = parts_of(jnp.concatenate(scalars, axis=1), 2)

    listed = jnp.broadcast_to(tile_row, (tiles, pairs)) == iota((tiles, pairs), 0)
    centre = pair_centres(cen_ref, halo_row)
    left = [jnp.where(listed, 1.0, 0.0).astype(BF16)]
    centre_parts = [part.astype(F32) for part in parts_of(centre, 2)]
    for part in centre_parts:
        for axis in range(3):
            value = jnp.broadcast_to(part[axis : axis + 1, :], (tiles, pairs))
            left.append(jnp.where(listed, value, 0.0).astype(BF16))
    left = jnp.concatenate(left, axis=0)
    from_high = bdot(left, high)
    from_low = bdot(left[: 4 * tiles], low)
    whole = from_high[:tiles] + from_low[:tiles]
    for axis in range(3):
        a, b = (1 + axis) * tiles, (4 + axis) * tiles
        pulled = from_high[a : a + tiles] + from_high[b : b + tiles] + from_low[a : a + tiles]
        out_ref[axis] = pos_ref[axis] * whole - pulled
    half = tiles // 2
    bit = lax.axis_index(halo_axis) % 2
    for ref, which in ((keep_ref, bit), (send_ref, 1 - bit)):
        first = pl.multiple_of(which * half, 8)
        for axis in range(3):
            block = out_ref[axis, pl.ds(first, half), :]
            for at in range(half):
                ref[axis : axis + 1, at * BLK : (at + 1) * BLK] = block[at : at + 1, :]


def butterfly(value, name, size, distance):
    return lax.ppermute(value, name, [(at, at ^ distance) for at in range(size)])


def per_device(
    n_space, n_halo,
    positions, masses, centres, pair_halo, pair_tile, halo_slot, feedback, mixing, drive, readout,
):
    knots = mixing.shape[1]
    particles = masses.shape[0]
    tiles = particles // BLK
    pairs = pair_halo.shape[1]
    halos = halo_slot.shape[1]
    rows = halos + 8 * pl.cdiv(halos // LANES, 8)
    vmem = pl.BlockSpec(memory_space=pltpu.VMEM)
    smem = pl.BlockSpec(memory_space=pltpu.SMEM)
    profile, u, places = pl.pallas_call(
        project_kernel,
        out_shape=(
            jax.ShapeDtypeStruct((rows, knots), F32),
            jax.ShapeDtypeStruct((pairs, BLK), F32),
            jax.ShapeDtypeStruct((3, tiles, BLK), F32),
        ),
        in_specs=[vmem] * 6 + [smem],
        out_specs=(vmem,) * 3,
        scratch_shapes=[pltpu.VMEM((pairs, BLK), F32), pltpu.VMEM((pairs, 2 * knots), F32)],
    )(
        positions, masses.reshape(particles // LANES, LANES), centres,
        pair_halo, pair_tile, halo_slot, feedback,
    )
    held, distance = [profile], 1
    while distance < n_space:
        total = sum(held[1:], held[0])
        if distance == 1 or distance * 2 == n_space:
            steps = [distance]
        else:
            steps = [distance, 2 * distance, 3 * distance]
        held = [total] + [butterfly(total, "space", n_space, step) for step in steps]
        distance *= 2 * len(steps) if len(steps) == 1 else 4
    keep, send = pl.pallas_call(
        functools.partial(relax_kernel, len(held), "halo"),
        out_shape=(jax.ShapeDtypeStruct((3, particles // 2), F32),) * 2,
        in_specs=[vmem] * (len(held) + 8),
        out_specs=(vmem,) * 2,
        scratch_shapes=[
            pltpu.VMEM((3, LANES, knots), F32),
            pltpu.VMEM((3, LANES, knots), F32),
            pltpu.VMEM((3, 2 * knots, 2 * knots), BF16),
            pltpu.VMEM((halos, 2 * knots), F32),
            pltpu.VMEM((3, tiles, BLK), F32),
        ],
    )(*held, u, places, centres, pair_halo, pair_tile, mixing, drive, readout)
    keep = keep + butterfly(send, "halo", n_halo, 1)
    distance = 2
    while distance < n_halo:
        keep = keep + butterfly(keep, "halo", n_halo, distance)
        distance *= 2
    other = butterfly(keep, "halo", n_halo, 1)
    first = lax.axis_index("halo") % 2 == 0
    return jnp.where(
        first, jnp.concatenate([keep, other], axis=1), jnp.concatenate([other, keep], axis=1)
    )


def solution(mesh):
    return jax.shard_map(
        functools.partial(per_device, mesh.shape["space"], mesh.shape["halo"]),
        mesh=mesh,
        in_specs=(
            P(None, "space"),
            P("space"),
            P("halo", None, None),
            P("halo", "space"),
            P("halo", "space"),
            P("halo", None),
            P("halo", "space"),
            P(),
            P(),
            P(),
        ),
        out_specs=P(None, "space"),
        check_vma=False,
    )
```

time: 230 us -> 44.4 us (0.19)
  other arithmetic: 86.2 us -> 2.64 us
  waiting for transfers between devices: 79.7 us -> 15.5 us
  blocking collectives: 23.2 us -> 0 us
  Pallas kernels: 0 us -> 14.7 us
  between operations: 14.5 us -> 0.05 us
  matrix products: 12.1 us -> 0 us
  local copies, waits for them, and re-layouts: 12.7 us -> 1.88 us
  starting transfers between devices: 0.04 us -> 9.36 us
    psum x2 -> x0, waiting for transfers between devices: 79.7 us -> none  [the longest x1 47.3 us: per_device(): lax.psum(jnp.dot(halo_selection, pair_rows, precision=lax.Precision.HIGHE...]
    reduce_sum x33 -> x0, other arithmetic: 77.8 us -> none  [the longest x8 39.8 us: project(): return jnp.sum(weight_part[:, :, None] * basis, axis=1)]
    unnamed x1 -> x0, blocking collectives: 23.2 us -> none
    ppermute x0 -> x7, waiting for transfers between devices: none -> 15.5 us  [butterfly(): lax.ppermute(value, name, [(at, at ^ distance) for at in range(size)])]
    pallas_call x0 -> x2, Pallas kernels: none -> 14.7 us  [the longest x1 9.3 us: per_device(): pl.pallas_call(project_kernel, out_shape=(jax.ShapeDtypeStruct((rows, kno...]
    dot_general x23 -> x0, matrix products: 12.1 us -> none  [the longest x21 9.13 us: relax(): mixed = jnp.dot(state[comp], mixing[comp], precision=lax.Precision.HIGHEST)]
    ppermute x0 -> x7, starting transfers between devices: none -> 9.36 us  [butterfly(): lax.ppermute(value, name, [(at, at ^ distance) for at in range(size)])]
    gather x6 -> x0, local copies, waits for them, and re-layouts: 7.79 us -> none  [the longest x3 4.22 us: per_device(): offsets = places[:, tile_ids, :] - centre_rows[:, halo_ids][:, :, None]]
  transfers between devices with their start and end apart: 2 -> 7, of which waited for: 2 -> 7; matrix products, arithmetic and copies ran while one was open for 0% -> 0% of each run, Pallas kernels for 0% -> 0%
where the time goes in v1:
time: 44.4 us; the launch traced here: 44.1 us
  waiting for transfers between devices  15.5 us (35%)
  Pallas kernels  14.7 us (33%)
  starting transfers between devices  9.36 us (21%)
  other arithmetic  2.64 us (6%)
  local copies, waits for them, and re-layouts  1.88 us (4%)
    ppermute x7, waiting for transfers between devices, butterfly(): lax.ppermute(value, name, [(at, at ^ distance) for at in range(size)])  15.5 us
    ppermute x7, starting transfers between devices, butterfly(): lax.ppermute(value, name, [(at, at ^ distance) for at in range(size)])  9.36 us
    pallas_call x1, Pallas kernels, per_device(): pl.pallas_call(project_kernel, out_shape=(jax.ShapeDtypeStruct((rows, kno...  9.3 us
    pallas_call x1, Pallas kernels, per_device(): pl.pallas_call(functools.partial(relax_kernel, len(held), 'halo'), out_sh...  5.36 us
    unnamed x9, local copies, waits for them, and re-layouts  1.88 us
    add x1, other arithmetic, per_device(): keep = keep + butterfly(send, 'halo', n_halo, 1)  0.94 us
    add x1, other arithmetic, per_device(): total = sum(held[1:], held[0])  0.9 us
  transfers between devices with their start and end apart: 7, of which 7 were waited for; matrix products, arithmetic and copies ran while one was open for 0% of the time, Pallas kernels for 0%

profile of v1, /device:TPU:0, one launch (start us, length us, event | category | flops | bytes accessed | tf_op | source)
XLA Modules:
  0.0 44.1 jit_solution(18277854875497830861)
XLA Ops:
  0.0 1.3 %copy.11.cen_ref.refs_6_ = f32[1,3,128]{2,1,0:T(4,128)} copy(f32[1,3,128]{2,0,1:T(1,128)} %param.12) | data formatting | bytes 3072 | tf_op args[2]
  1.3 9.3 %shard_map.100 = (f32[136,128]{1,0:T(8,128)}, f32[256,512]{1,0:T(8,128)}, f32[3,32,512]{2,1,0:T(8,128)}) custom-call(f32[3,16384]{1,0:T(4,128)} %pos_ref.1, f32[128,128]{1,0:T(8,128)} %bitcast.1, f32[1,3,128]{2,1,0:T(4,128)} %copy.11.cen_ref.refs_6_, s32[1,256]{1,0:T(1,128)} %refs_7_.1, s32[1,256]{1,0:T(1,128)} %refs_8_.1, s32[1,128]{1,0:T(1,128)} %slot_ref.1, ...), custom_call_target="tpu_custom_call" | custom-call | tf_op jit(solution)/shard_map/pallas_call | solution.py:240
  10.6 3.0 %collective-permute-start = (f32[136,128]{1,0:T(8,128)}, f32[136,128]{1,0:T(8,128)S(1)}, u32[]{:S(2)}, u32[]{:S(2)}) collective-permute-start(f32[136,128]{1,0:T(8,128)} %get-tuple-element.10), channel_id=1, source_target_pairs={{0,4},{4,0},{8,12},{12,8},{16,20},{20,16},{24,28},{28,24},{1,5},{5... | collective-permute-start | bytes 208904 | tf_op jit(solution)/shard_map/ppermute | solution.py:225
  13.6 2.5 %collective-permute-done = f32[136,128]{1,0:T(8,128)S(1)} collective-permute-done((f32[136,128]{1,0:T(8,128)}, f32[136,128]{1,0:T(8,128)S(1)}, u32[]{:S(2)}, u32[]{:S(2)}) %collective-permute-start) | collective-permute-done | bytes 69664 | tf_op jit(solution)/shard_map/ppermute | solution.py:225
  16.1 0.9 %add.14.refs_0_ = f32[136,128]{1,0:T(8,128)S(1)} add(f32[136,128]{1,0:T(8,128)} %get-tuple-element.10, f32[136,128]{1,0:T(8,128)S(1)} %collective-permute-done) | non-fusion elementwise | flops 17408 | bytes 208896 | tf_op jit(solution)/shard_map/add | solution.py:256
  17.0 2.1 %collective-permute-start.1 = (f32[136,128]{1,0:T(8,128)S(1)}, f32[136,128]{1,0:T(8,128)S(1)}, u32[]{:S(2)}, u32[]{:S(2)}) collective-permute-start(f32[136,128]{1,0:T(8,128)S(1)} %add.14.refs_0_), channel_id=1, source_target_pairs={{0,8},{4,12},{8,0},{12,4},{16,24},{20,28},{24,16},{28,20},{1,9},{5... | collective-permute-start | bytes 208904 | tf_op jit(solution)/shard_map/ppermute | solution.py:225
  19.1 2.6 %collective-permute-start.2 = (f32[136,128]{1,0:T(8,128)S(1)}, f32[136,128]{1,0:T(8,128)S(1)}, u32[]{:S(2)}, u32[]{:S(2)}) collective-permute-start(f32[136,128]{1,0:T(8,128)S(1)} %add.14.refs_0_), channel_id=1, source_target_pairs={{0,16},{4,20},{8,24},{12,28},{16,0},{20,4},{24,8},{28,12},{1,17},{... | collective-permute-start | bytes 208904 | tf_op jit(solution)/shard_map/ppermute | solution.py:225
  21.7 0.0 collective-permute-start.3
  21.7 0.4 collective-permute-done.1.refs_1_
  22.1 3.7 %collective-permute-done.2.refs_2_ = f32[136,128]{1,0:T(8,128)S(1)} collective-permute-done((f32[136,128]{1,0:T(8,128)S(1)}, f32[136,128]{1,0:T(8,128)S(1)}, u32[]{:S(2)}, u32[]{:S(2)}) %collective-permute-start.2) | collective-permute-done | bytes 69664 | tf_op jit(solution)/shard_map/ppermute | solution.py:225
  25.8 2.0 %collective-permute-done.3.refs_3_ = f32[136,128]{1,0:T(8,128)S(1)} collective-permute-done((f32[136,128]{1,0:T(8,128)S(1)}, f32[136,128]{1,0:T(8,128)S(1)}, u32[]{:S(2)}, u32[]{:S(2)}) %collective-permute-start.3) | collective-permute-done | bytes 69664 | tf_op jit(solution)/shard_map/ppermute | solution.py:225
  27.8 0.0 copy-done
  27.8 0.0 copy-done.1
  27.8 0.0 copy-done.2
  27.8 0.6 %copy-done.3 = f32[136,128]{1,0:T(8,128)} copy-done((f32[136,128]{1,0:T(8,128)}, f32[136,128]{1,0:T(8,128)S(1)}, u32[]{:S(2)}) %copy-start.3) | copy-done | bytes 69656
  28.4 5.4 %shard_map.101 = (f32[3,8192]{1,0:T(4,128)}, f32[3,8192]{1,0:T(4,128)}) custom-call(f32[136,128]{1,0:T(8,128)} %copy-done, f32[136,128]{1,0:T(8,128)} %copy-done.1, f32[136,128]{1,0:T(8,128)} %copy-done.2, f32[136,128]{1,0:T(8,128)} %copy-done.3, f32[256,512]{1,0:T(8,128)} %get-tuple-element.11.refs_4_, f32[3,32,512]{2,1,0:T(8,128)} %get-tuple-element.12.refs_5_, ...), custom_call_target="tpu_custom_call" | custom-call | tf_op jit(solution)/shard_map/pallas_call | solution.py:263
  33.8 0.0 collective-permute-start.4
  33.8 1.6 %collective-permute-done.4 = f32[3,8192]{1,0:T(4,128)S(1)} collective-permute-done((f32[3,8192]{1,0:T(4,128)}, f32[3,8192]{1,0:T(4,128)S(1)}, u32[]{:S(2)}, u32[]{:S(2)}) %collective-permute-start.4) | collective-permute-done | bytes 98336 | tf_op jit(solution)/shard_map/ppermute | solution.py:225
  35.3 0.9 %add.15 = f32[3,8192]{1,0:T(4,128)S(1)} add(f32[3,8192]{1,0:T(4,128)} %get-tuple-element.13, f32[3,8192]{1,0:T(4,128)S(1)} %collective-permute-done.4) | non-fusion elementwise | flops 24576 | bytes 294912 | tf_op jit(solution)/shard_map/add | solution.py:276
  36.3 1.6 %collective-permute-start.5 = (f32[3,8192]{1,0:T(4,128)S(1)}, f32[3,8192]{1,0:T(4,128)S(1)}, u32[]{:S(2)}, u32[]{:S(2)}) collective-permute-start(f32[3,8192]{1,0:T(4,128)S(1)} %add.15), channel_id=1, source_target_pairs={{0,2},{1,3},{2,0},{3,1},{4,6},{5,7},{6,4},{7,5},{8,10},{9,11},{10,... | collective-permute-start | bytes 294920 | tf_op jit(solution)/shard_map/ppermute | solution.py:225
  37.8 4.1 %collective-permute-done.5 = f32[3,8192]{1,0:T(4,128)S(1)} collective-permute-done((f32[3,8192]{1,0:T(4,128)S(1)}, f32[3,8192]{1,0:T(4,128)S(1)}, u32[]{:S(2)}, u32[]{:S(2)}) %collective-permute-start.5) | collective-permute-done | bytes 98336 | tf_op jit(solution)/shard_map/ppermute | solution.py:225
  41.9 0.1 collective-permute-start.6
  42.0 1.3 %collective-permute-done.6 = f32[3,8192]{1,0:T(4,128)S(1)} collective-permute-done((f32[3,8192]{1,0:T(4,128)S(1)}, f32[3,8192]{1,0:T(4,128)S(1)}, u32[]{:S(2)}, u32[]{:S(2)}) %collective-permute-start.6) | collective-permute-done | bytes 98336 | tf_op jit(solution)/shard_map/ppermute | solution.py:225
  43.4 0.8 %maximum_select_fusion = f32[3,16384]{1,0:T(4,128)} fusion(f32[3,8192]{1,0:T(4,128)S(1)} %collective-permute-done.6, f32[3,8192]{1,0:T(4,128)S(1)} %add.16, pred[]{:T(512)S(6)} %eq.5), kind=kLoop, calls=%fused_computation | loop fusion | flops 147456 | bytes 393217 | tf_op jit(solution)/shard_map/jit(_where)/select_n | solution.py:283
  (5 shorter events, 0.0 us)
Async XLA Ops:
  10.6 5.5 %collective-permute-start = (f32[136,128]{1,0:T(8,128)}, f32[136,128]{1,0:T(8,128)S(1)}, u32[]{:S(2)}, u32[]{:S(2)}) collective-permute-start(f32[136,128]{1,0:T(8,128)} %get-tuple-element.10), channel_id=1, source_target_pairs={{0,4},{4,0},{8,12},{12,8},{16,20},{20,16},{24,28},{28,24},{1,5},{5... | collective-permute-start | bytes 208904 | tf_op jit(solution)/shard_map/ppermute | solution.py:225
  17.0 10.9 %copy-start = (f32[136,128]{1,0:T(8,128)}, f32[136,128]{1,0:T(8,128)S(1)}, u32[]{:S(2)}) copy-start(f32[136,128]{1,0:T(8,128)S(1)} %add.14.refs_0_) | copy-start | bytes 208900
  17.0 5.1 %collective-permute-start.1 = (f32[136,128]{1,0:T(8,128)S(1)}, f32[136,128]{1,0:T(8,128)S(1)}, u32[]{:S(2)}, u32[]{:S(2)}) collective-permute-start(f32[136,128]{1,0:T(8,128)S(1)} %add.14.refs_0_), channel_id=1, source_target_pairs={{0,8},{4,12},{8,0},{12,4},{16,24},{20,28},{24,16},{28,20},{1,9},{5... | collective-permute-start | bytes 208904 | tf_op jit(solution)/shard_map/ppermute | solution.py:225
  19.1 6.7 %collective-permute-start.2 = (f32[136,128]{1,0:T(8,128)S(1)}, f32[136,128]{1,0:T(8,128)S(1)}, u32[]{:S(2)}, u32[]{:S(2)}) collective-permute-start(f32[136,128]{1,0:T(8,128)S(1)} %add.14.refs_0_), channel_id=1, source_target_pairs={{0,16},{4,20},{8,24},{12,28},{16,0},{20,4},{24,8},{28,12},{1,17},{... | collective-permute-start | bytes 208904 | tf_op jit(solution)/shard_map/ppermute | solution.py:225
  21.7 6.1 %collective-permute-start.3 = (f32[136,128]{1,0:T(8,128)S(1)}, f32[136,128]{1,0:T(8,128)S(1)}, u32[]{:S(2)}, u32[]{:S(2)}) collective-permute-start(f32[136,128]{1,0:T(8,128)S(1)} %add.14.refs_0_), channel_id=1, source_target_pairs={{0,24},{4,28},{8,16},{12,20},{16,8},{20,12},{24,0},{28,4},{1,25},{... | collective-permute-start | bytes 208904 | tf_op jit(solution)/shard_map/ppermute | solution.py:225
  22.1 5.7 %copy-start.1 = (f32[136,128]{1,0:T(8,128)}, f32[136,128]{1,0:T(8,128)S(1)}, u32[]{:S(2)}) copy-start(f32[136,128]{1,0:T(8,128)S(1)} %collective-permute-done.1.refs_1_) | copy-start | bytes 208900
  25.8 2.0 %copy-start.2 = (f32[136,128]{1,0:T(8,128)}, f32[136,128]{1,0:T(8,128)S(1)}, u32[]{:S(2)}) copy-start(f32[136,128]{1,0:T(8,128)S(1)} %collective-permute-done.2.refs_2_) | copy-start | bytes 208900
  27.8 0.6 %copy-start.3 = (f32[136,128]{1,0:T(8,128)}, f32[136,128]{1,0:T(8,128)S(1)}, u32[]{:S(2)}) copy-start(f32[136,128]{1,0:T(8,128)S(1)} %collective-permute-done.3.refs_3_) | copy-start | bytes 208900
  33.8 1.6 %collective-permute-start.4 = (f32[3,8192]{1,0:T(4,128)}, f32[3,8192]{1,0:T(4,128)S(1)}, u32[]{:S(2)}, u32[]{:S(2)}) collective-permute-start(f32[3,8192]{1,0:T(4,128)} %get-tuple-element.14), channel_id=1, source_target_pairs={{0,1},{1,0},{2,3},{3,2},{4,5},{5,4},{6,7},{7,6},{8,9},{9,8},{10,11... | collective-permute-start | bytes 294920 | tf_op jit(solution)/shard_map/ppermute | solution.py:225
  36.3 5.6 %collective-permute-start.5 = (f32[3,8192]{1,0:T(4,128)S(1)}, f32[3,8192]{1,0:T(4,128)S(1)}, u32[]{:S(2)}, u32[]{:S(2)}) collective-permute-start(f32[3,8192]{1,0:T(4,128)S(1)} %add.15), channel_id=1, source_target_pairs={{0,2},{1,3},{2,0},{3,1},{4,6},{5,7},{6,4},{7,5},{8,10},{9,11},{10,... | collective-permute-start | bytes 294920 | tf_op jit(solution)/shard_map/ppermute | solution.py:225
  41.9 1.4 %collective-permute-start.6 = (f32[3,8192]{1,0:T(4,128)S(1)}, f32[3,8192]{1,0:T(4,128)S(1)}, u32[]{:S(2)}, u32[]{:S(2)}) collective-permute-start(f32[3,8192]{1,0:T(4,128)S(1)} %add.16), channel_id=1, source_target_pairs={{0,1},{1,0},{2,3},{3,2},{4,5},{5,4},{6,7},{7,6},{8,9},{9,8},{10,11... | collective-permute-start | bytes 294920 | tf_op jit(solution)/shard_map/ppermute | solution.py:225

commit v2 on v1

v2 whole, which is shorter than its diff:
```python
import functools

import jax
import jax.numpy as jnp
from jax import lax
from jax.experimental import pallas as pl
from jax.experimental.pallas import tpu as pltpu
from jax.sharding import PartitionSpec as P

BLK = 512
ITERS = 8
LANES = 128
PACK = 16
UNROLL = 8
ROOM = 24 << 20
F32, BF16 = jnp.float32, jnp.bfloat16


def iota(shape, axis):
    return lax.broadcasted_iota(jnp.int32, shape, axis)


def parts_of(value, count):
    parts = []
    for at in range(count):
        parts.append(value.astype(BF16))
        if at + 1 < count:
            value = value - parts[-1].astype(F32)
    return parts


def bdot(a, b):
    return lax.dot_general(a, b, (((1,), (0,)), ((), ())), preferred_element_type=F32)


def bdot_t(a, b):
    return lax.dot_general(a, b, (((1,), (1,)), ((), ())), preferred_element_type=F32)


def lane_gather(table, index):
    return jnp.take_along_axis(table, index, axis=1, mode="promise_in_bounds")


def pair_centres(cen_ref, halo_row):
    pairs, halos = halo_row.shape[1], cen_ref.shape[2]
    cen = jnp.concatenate([cen_ref[0], cen_ref[1], cen_ref[2], jnp.zeros((5, halos), F32)], axis=0)
    blocks = []
    for at in range(pairs // LANES):
        ids = jnp.broadcast_to(halo_row[:, at * LANES : (at + 1) * LANES], (8, LANES))
        found = jnp.zeros((8, LANES), F32)
        for block in range(halos // LANES):
            here = lane_gather(cen[:, block * LANES : (block + 1) * LANES], ids & (LANES - 1))
            found = jnp.where((ids >> 7) == block, here, found)
        blocks.append(found)
    return jnp.concatenate(blocks, axis=1)


def project_kernel(
    pos_hbm, mass_hbm, cen_hbm, halo_hbm, tile_hbm, slot_hbm, feed_hbm,
    out_ref, u_ref,
    pos_ref, mass_ref, cen_ref, halo_ref, tile_ref, slot_ref, feed_ref,
    place_ref, m_ref, spread_ref, sems,
):
    sources = (halo_hbm, tile_hbm, cen_hbm, pos_hbm, mass_hbm, slot_hbm, feed_hbm)
    targets = (halo_ref, tile_ref, cen_ref, pos_ref, mass_ref, slot_ref, feed_ref)
    copies = [
        pltpu.make_async_copy(source, target, sems.at[at])
        for at, (source, target) in enumerate(zip(sources, targets))
    ]
    for copy in copies:
        copy.start()
    pairs, halos = halo_ref.shape[1], slot_ref.shape[1]
    tiles = place_ref.shape[1]
    knots = out_ref.shape[1]
    chunks = BLK // LANES
    scale = (knots - 1) / 2.6
    for copy in copies[:3]:
        copy.wait()
    centre = pair_centres(cen_ref, halo_ref[...]) * scale
    select = jnp.broadcast_to(tile_ref[...], (tiles, pairs)) == iota((tiles, pairs), 0)
    select = jnp.where(select, 1.0, 0.0)
    centre = [part.astype(F32) for part in parts_of(centre, 3)]
    pad = jnp.zeros((LANES - 3 * tiles - 24, pairs), F32)
    select = jnp.transpose(jnp.concatenate([select] * 3 + centre + [pad], axis=0)).astype(BF16)
    shape = (LANES - 3 * tiles, 4 * BLK)
    less = (iota(shape, 0) < 24) & ((iota(shape, 0) & 7) == iota(shape, 1) // BLK)
    less = jnp.where(less & (iota(shape, 1) < 3 * BLK), -1.0, 0.0).astype(BF16)
    for copy in copies[3:5]:
        copy.wait()
    for tile in range(tiles):
        block = pos_ref[:, tile * BLK : (tile + 1) * BLK]
        for axis in range(3):
            place_ref[axis, tile : tile + 1, :] = block[axis : axis + 1, :]
    mass = jnp.concatenate(
        [mass_ref[pl.ds(at, tiles, stride=chunks), :] for at in range(chunks)], axis=1
    )
    table = [place_ref[axis] * scale for axis in range(3)] + [mass]
    table = jnp.concatenate([jnp.concatenate(parts_of(t, 3), axis=0) for t in table], axis=1)
    found = bdot(select, jnp.concatenate([table, less], axis=0))
    square = sum(found[:, axis * BLK : (axis + 1) * BLK] ** 2 for axis in range(3))
    u_ref[...] = square * lax.rsqrt(jnp.maximum(square, 1e-30))
    m_ref[...] = found[:, 3 * BLK :]
    for copy in copies[5:]:
        copy.wait()

    lows = 2 * LANES // PACK
    highs = knots // lows
    wide = LANES // PACK
    lane = iota((PACK, LANES), 1)
    index = (lane % wide) * PACK + iota((PACK, LANES), 0)
    window = lane // wide

    def group(at, carry):
        rows = pl.ds(pl.multiple_of(at * PACK, PACK), PACK)
        u = u_ref[rows, :]
        m = m_ref[rows, :]
        whole = jnp.floor(u)
        after = m * (u - whole)
        high = jnp.floor(whole * (1.0 / lows))
        low = (whole - high * lows).astype(BF16)
        high = high.astype(BF16)
        zero = jnp.zeros(u.shape, BF16)
        one = jnp.ones(u.shape, BF16)
        values = parts_of(m - after, 2) + parts_of(after, 2)
        left = jnp.concatenate(
            [jnp.where(high == h, v, zero) for v in values for h in range(highs)], axis=0
        )
        right = jnp.concatenate([jnp.where(low == b, one, zero) for b in range(lows)], axis=0)
        both = bdot_t(left, right)
        for which in range(2):
            spread = jnp.zeros((PACK, knots), F32)
            for h in range(highs):
                first = ((2 * which) * highs + h) * PACK
                other = ((2 * which + 1) * highs + h) * PACK
                tile = both[first : first + PACK] + both[other : other + PACK]
                for half in range(2):
                    here = lane_gather(tile[:, half * LANES : (half + 1) * LANES], index)
                    spread = jnp.where(window == 2 * h + half, here, spread)
            spread_ref[rows, which * knots : (which + 1) * knots] = spread
        return carry

    lax.fori_loop(0, pairs // PACK, group, 0, unroll=UNROLL)

    owner = jnp.broadcast_to(halo_ref[...], (halos, pairs)) == iota((halos, pairs), 0)
    owner = jnp.where(owner, 1.0, 0.0).astype(BF16)
    total = sum(bdot(owner, part) for part in parts_of(spread_ref[...], 2))
    out_ref[:halos, :] = total[:, :knots] + pltpu.roll(total[:, knots:], 1, 1)

    mine = feed_ref.shape[1]
    slot = slot_ref[...] - lax.axis_index("space") * mine
    phi = jnp.zeros((1, halos), F32)
    for at in range(mine):
        phi = jnp.where(slot == at, feed_ref[0, at], phi)
    out_ref[halos:, :] = jnp.zeros((out_ref.shape[0] - halos, knots), F32)
    for at in range(halos // LANES):
        out_ref[halos + at : halos + at + 1, :] = phi[:, at * LANES : (at + 1) * LANES]


def relax_kernel(count, halo_axis, *refs):
    profile_refs = refs[:count]
    (
        u_ref, pos_ref, cen_ref, halo_ref, tile_ref, mix_ref, drive_ref, readout_ref,
        keep_ref, send_ref, state_ref, base_ref, weight_ref, table_ref, sum_ref,
    ) = refs[count:]
    pairs, halos = halo_ref.shape[1], cen_ref.shape[2]
    tiles, knots = pos_ref.shape[1] // BLK, drive_ref.shape[1]
    for comp in range(3):
        high, low = parts_of(mix_ref[comp], 2)
        both = jnp.concatenate([high, low], axis=1)
        weight_ref[comp] = jnp.concatenate([both, both], axis=0)
    extra = sum(ref[halos:, :] for ref in profile_refs)
    phi_columns = jnp.transpose(extra)
    for block in range(halos // LANES):
        rows = slice(block * LANES, (block + 1) * LANES)
        level = jnp.log1p(sum(ref[rows, :] for ref in profile_refs))
        phi = phi_columns[:, block : block + 1]
        for comp in range(3):
            base = drive_ref[comp : comp + 1, :] * level
            base_ref[comp] = base
            state_ref[comp] = jnp.tanh(base)

        def step(at, carry):
            old = [state_ref[comp] for comp in range(3)]
            half_mean = (old[0] + old[1] + old[2]) * (0.5 / 3.0)
            for comp in range(3):
                split = jnp.concatenate(parts_of(old[comp], 2), axis=1)
                mixed = bdot(split, weight_ref[comp])
                mixed = mixed[:, :knots] + mixed[:, knots:]
                state_ref[comp] = jnp.tanh(base_ref[comp] + phi * mixed + half_mean)
            return carry

        lax.fori_loop(0, ITERS - 1, step, 0)
        coef = sum(state_ref[comp] * readout_ref[comp : comp + 1, :] for comp in range(3))
        table_ref[rows, :knots] = coef
        table_ref[rows, knots:] = pltpu.roll(coef, knots - 1, 1) - coef

    halo_row, tile_row = halo_ref[...], tile_ref[...]
    halo_column = jnp.transpose(jnp.broadcast_to(halo_row, (8, pairs)).astype(F32))[:, :1]
    owner = jnp.where(halo_column.astype(jnp.int32) == iota((pairs, halos), 1), 1.0, 0.0).astype(BF16)
    tables = sum(bdot(owner, part) for part in parts_of(table_ref[...], 2))
    centre = pair_centres(cen_ref, halo_row)
    high, low = [part.astype(F32) for part in parts_of(centre, 2)]
    kinds = jnp.concatenate([high[:3], jnp.ones((1, pairs), F32), low[:4]], axis=0)
    tile_row = jnp.broadcast_to(tile_row, (8, pairs))
    left = jnp.concatenate([jnp.where(tile_row == at, kinds, 0.0) for at in range(tiles)], axis=0)
    left = left.astype(BF16)
    for at in range(BLK // LANES):
        u = u_ref[:, at * LANES : (at + 1) * LANES]
        whole = jnp.floor(u)
        index = whole.astype(jnp.int32)
        start = lane_gather(tables[:, :knots], index)
        slope = lane_gather(tables[:, knots:], index)
        high, low = parts_of(start + (u - whole) * slope, 2)
        sum_ref[:, at * LANES : (at + 1) * LANES] = bdot(left, high) + bdot(left, low)
    half = tiles // 2
    bit = lax.axis_index(halo_axis) & 1
    for ref, which in ((keep_ref, bit), (send_ref, 1 - bit)):
        for at in range(half):
            tile = which * half + at
            rows = sum_ref[pl.ds(pl.multiple_of(tile * 8, 8), 8), :]
            pos = pos_ref[:, pl.ds(pl.multiple_of(tile * BLK, BLK), BLK)]
            ref[:, at * BLK : (at + 1) * BLK] = pos * rows[3:4] - rows[:3] - rows[4:7]


def butterfly(value, name, size, distance):
    return lax.ppermute(value, name, [(at, at ^ distance) for at in range(size)])


def per_device(
    n_space, n_halo,
    positions, masses, centres, pair_halo, pair_tile, halo_slot, feedback, mixing, drive, readout,
):
    knots = mixing.shape[1]
    particles = masses.shape[0]
    tiles = particles // BLK
    pairs = pair_halo.shape[1]
    halos = halo_slot.shape[1]
    rows = halos + 8 * pl.cdiv(halos // LANES, 8)
    centres = jnp.transpose(centres, (1, 0, 2))
    room = pltpu.CompilerParams(vmem_limit_bytes=ROOM)
    vmem = pl.BlockSpec(memory_space=pltpu.VMEM)
    hbm = pl.BlockSpec(memory_space=pltpu.HBM)
    profile, u = pl.pallas_call(
        project_kernel,
        out_shape=(
            jax.ShapeDtypeStruct((rows, knots), F32),
            jax.ShapeDtypeStruct((pairs, BLK), F32),
        ),
        in_specs=[hbm] * 7,
        out_specs=(vmem,) * 2,
        scratch_shapes=[
            pltpu.VMEM(positions.shape, F32),
            pltpu.VMEM((particles // LANES, LANES), F32),
            pltpu.VMEM(centres.shape, F32),
            pltpu.VMEM(pair_halo.shape, jnp.int32),
            pltpu.VMEM(pair_tile.shape, jnp.int32),
            pltpu.VMEM(halo_slot.shape, jnp.int32),
            pltpu.SMEM(feedback.shape, F32),
            pltpu.VMEM((3, tiles, BLK), F32),
            pltpu.VMEM((pairs, BLK), F32),
            pltpu.VMEM((pairs, 2 * knots), F32),
            pltpu.SemaphoreType.DMA((7,)),
        ],
        compiler_params=room,
    )(
        *[
            pltpu.with_memory_space_constraint(value, pltpu.HBM)
            for value in (
                positions, masses.reshape(particles // LANES, LANES), centres,
                pair_halo, pair_tile, halo_slot, feedback,
            )
        ]
    )
    held, distance = [profile], 1
    while distance < n_space:
        total = sum(held[1:], held[0])
        if distance == 1 or distance * 2 == n_space:
            steps = [distance]
        else:
            steps = [distance, 2 * distance, 3 * distance]
        held = [total] + [butterfly(total, "space", n_space, step) for step in steps]
        distance *= 2 * len(steps) if len(steps) == 1 else 4
    keep, send = pl.pallas_call(
        functools.partial(relax_kernel, len(held), "halo"),
        out_shape=(jax.ShapeDtypeStruct((3, particles // 2), F32),) * 2,
        in_specs=[vmem] * (len(held) + 8),
        out_specs=(vmem,) * 2,
        scratch_shapes=[
            pltpu.VMEM((3, LANES, knots), F32),
            pltpu.VMEM((3, LANES, knots), F32),
            pltpu.VMEM((3, 2 * knots, 2 * knots), BF16),
            pltpu.VMEM((halos, 2 * knots), F32),
            pltpu.VMEM((8 * tiles, BLK), F32),
        ],
        compiler_params=room,
    )(*held, u, positions, centres, pair_halo, pair_tile, mixing, drive, readout)
    keep = keep + butterfly(send, "halo", n_halo, 1)
    distance = 2
    while distance < n_halo:
        keep = keep + butterfly(keep, "halo", n_halo, distance)
        distance *= 2
    other = butterfly(keep, "halo", n_halo, 1)
    first = lax.axis_index("halo") % 2 == 0
    return jnp.where(
        first, jnp.concatenate([keep, other], axis=1), jnp.concatenate([other, keep], axis=1)
    )


def solution(mesh):
    return jax.shard_map(
        functools.partial(per_device, mesh.shape["space"], mesh.shape["halo"]),
        mesh=mesh,
        in_specs=(
            P(None, "space"),
            P("space"),
            P("halo", None, None),
            P("halo", "space"),
            P("halo", "space"),
            P("halo", None),
            P("halo", "space"),
            P(),
            P(),
            P(),
        ),
        out_specs=P(None, "space"),
        check_vma=False,
    )
```

time: 44.4 us -> 33.6 us (0.76)
  Pallas kernels: 14.7 us -> 7.92 us
  local copies, waits for them, and re-layouts: 1.88 us -> 0.03 us
  other arithmetic: 2.64 us -> 0.84 us
    pallas_call x1, Pallas kernels: 9.3 us -> 4.71 us  [per_device(): pl.pallas_call(project_kernel, out_shape=(jax.ShapeDtypeStruct((rows, kno...]
    pallas_call x1, Pallas kernels: 5.36 us -> 3.21 us  [per_device(): pl.pallas_call(functools.partial(relax_kernel, len(held), 'halo'), out_sh...]
    unnamed x9 -> x14, local copies, waits for them, and re-layouts: 1.88 us -> 0.03 us
    add x1, other arithmetic: 0.94 us -> 0.04 us  [per_device(): keep = keep + butterfly(send, 'halo', n_halo, 1)]
    add x1, other arithmetic: 0.9 us -> 0.01 us  [per_device(): total = sum(held[1:], held[0])]
where the time goes in v2:
time: 33.6 us; the launch traced here: 33.5 us
  waiting for transfers between devices  15.1 us (45%)
  starting transfers between devices  9.49 us (28%)
  Pallas kernels  7.92 us (24%)
  other arithmetic  0.84 us (2%)
    ppermute x7, waiting for transfers between devices, butterfly(): lax.ppermute(value, name, [(at, at ^ distance) for at in range(size)])  15.1 us
    ppermute x7, starting transfers between devices, butterfly(): lax.ppermute(value, name, [(at, at ^ distance) for at in range(size)])  9.49 us
    pallas_call x1, Pallas kernels, per_device(): pl.pallas_call(project_kernel, out_shape=(jax.ShapeDtypeStruct((rows, kno...  4.71 us
    pallas_call x1, Pallas kernels, per_device(): pl.pallas_call(functools.partial(relax_kernel, len(held), 'halo'), out_sh...  3.21 us
    select_n x1, other arithmetic, per_device(): jnp.where(first, jnp.concatenate([keep, other], axis=1), jnp.concatenate(...  0.76 us
  transfers between devices with their start and end apart: 7, of which 7 were waited for; matrix products, arithmetic and copies ran while one was open for 0% of the time, Pallas kernels for 0%

profile of v2, /device:TPU:0, one launch (start us, length us, event | category | flops | bytes accessed | tf_op | source)
XLA Modules:
  0.0 33.5 jit_solution(2904586584481986142)
XLA Ops:
  0.0 4.7 %shard_map.100 = (f32[136,128]{1,0:T(8,128)S(1)}, f32[256,512]{1,0:T(8,128)S(1)}) custom-call(f32[3,16384]{1,0:T(4,128)} %refs_5_.1, f32[128,128]{1,0:T(8,128)} %bitcast.4, f32[3,1,128]{2,1,0:T(1,128)} %bitcast.2, s32[1,256]{1,0:T(1,128)} %refs_7_.1, s32[1,256]{1,0:T(1,128)} %refs_8_.1, s32[1,128]{1,0:T(1,128)} %slot_hbm.1, f32[1,16]{1,0:T(1,128)} %feed_hbm.1), custom_call_target="tpu_custom_call" | custom-call | tf_op jit(solution)/shard_map/pallas_call | solution.py:243
  4.7 3.1 %collective-permute-start = (f32[136,128]{1,0:T(8,128)S(1)}, f32[136,128]{1,0:T(8,128)S(1)}, u32[]{:S(2)}, u32[]{:S(2)}) collective-permute-start(f32[136,128]{1,0:T(8,128)S(1)} %get-tuple-element.9), channel_id=1, source_target_pairs={{0,4},{4,0},{8,12},{12,8},{16,20},{20,16},{24,28},{28,24},{1,5},{5... | collective-permute-start | bytes 208904 | tf_op jit(solution)/shard_map/ppermute | solution.py:226
  7.8 2.3 %collective-permute-done = f32[136,128]{1,0:T(8,128)S(1)} collective-permute-done((f32[136,128]{1,0:T(8,128)S(1)}, f32[136,128]{1,0:T(8,128)S(1)}, u32[]{:S(2)}, u32[]{:S(2)}) %collective-permute-start) | collective-permute-done | bytes 69664 | tf_op jit(solution)/shard_map/ppermute | solution.py:226
  10.1 0.0 copy-start.2
  10.1 2.1 %collective-permute-start.1 = (f32[136,128]{1,0:T(8,128)S(1)}, f32[136,128]{1,0:T(8,128)S(1)}, u32[]{:S(2)}, u32[]{:S(2)}) collective-permute-start(f32[136,128]{1,0:T(8,128)S(1)} %add.14.refs_0_), channel_id=1, source_target_pairs={{0,8},{4,12},{8,0},{12,4},{16,24},{20,28},{24,16},{28,20},{1,9},{5... | collective-permute-start | bytes 208904 | tf_op jit(solution)/shard_map/ppermute | solution.py:226
  12.3 2.6 %collective-permute-start.2 = (f32[136,128]{1,0:T(8,128)S(1)}, f32[136,128]{1,0:T(8,128)S(1)}, u32[]{:S(2)}, u32[]{:S(2)}) collective-permute-start(f32[136,128]{1,0:T(8,128)S(1)} %add.14.refs_0_), channel_id=1, source_target_pairs={{0,16},{4,20},{8,24},{12,28},{16,0},{20,4},{24,8},{28,12},{1,17},{... | collective-permute-start | bytes 208904 | tf_op jit(solution)/shard_map/ppermute | solution.py:226
  14.8 0.0 collective-permute-start.3
  14.8 0.4 %collective-permute-done.1.refs_1_ = f32[136,128]{1,0:T(8,128)S(1)} collective-permute-done((f32[136,128]{1,0:T(8,128)S(1)}, f32[136,128]{1,0:T(8,128)S(1)}, u32[]{:S(2)}, u32[]{:S(2)}) %collective-permute-start.1) | collective-permute-done | bytes 69664 | tf_op jit(solution)/shard_map/ppermute | solution.py:226
  15.2 3.7 %collective-permute-done.2.refs_2_ = f32[136,128]{1,0:T(8,128)S(1)} collective-permute-done((f32[136,128]{1,0:T(8,128)S(1)}, f32[136,128]{1,0:T(8,128)S(1)}, u32[]{:S(2)}, u32[]{:S(2)}) %collective-permute-start.2) | collective-permute-done | bytes 69664 | tf_op jit(solution)/shard_map/ppermute | solution.py:226
  19.0 2.0 %collective-permute-done.3.refs_3_ = f32[136,128]{1,0:T(8,128)S(1)} collective-permute-done((f32[136,128]{1,0:T(8,128)S(1)}, f32[136,128]{1,0:T(8,128)S(1)}, u32[]{:S(2)}, u32[]{:S(2)}) %collective-permute-start.3) | collective-permute-done | bytes 69664 | tf_op jit(solution)/shard_map/ppermute | solution.py:226
  20.9 0.0 copy-done
  20.9 0.0 copy-done.1
  21.0 0.0 copy-done.3
  21.0 0.0 copy-done.4
  21.0 0.0 copy-done.5
  21.0 0.0 copy-done.6
  21.0 3.2 %shard_map.101 = (f32[3,8192]{1,0:T(4,128)S(1)}, f32[3,8192]{1,0:T(4,128)S(1)}) custom-call(f32[136,128]{1,0:T(8,128)S(1)} %add.14.refs_0_, f32[136,128]{1,0:T(8,128)S(1)} %collective-permute-done.1.refs_1_, f32[136,128]{1,0:T(8,128)S(1)} %collective-permute-done.2.refs_2_, f32[136,128]{1,0:T(8,128)S(1)} %collective-permute-done.3.refs_3_, ...), custom_call_target="tpu_custom_call" | custom-call | tf_op jit(solution)/shard_map/pallas_call | solution.py:283
  24.2 0.1 collective-permute-start.4
  24.3 1.3 %collective-permute-done.4 = f32[3,8192]{1,0:T(4,128)S(1)} collective-permute-done((f32[3,8192]{1,0:T(4,128)S(1)}, f32[3,8192]{1,0:T(4,128)S(1)}, u32[]{:S(2)}, u32[]{:S(2)}) %collective-permute-start.4) | collective-permute-done | bytes 98336 | tf_op jit(solution)/shard_map/ppermute | solution.py:226
  25.7 1.6 %collective-permute-start.5 = (f32[3,8192]{1,0:T(4,128)S(1)}, f32[3,8192]{1,0:T(4,128)S(1)}, u32[]{:S(2)}, u32[]{:S(2)}) collective-permute-start(f32[3,8192]{1,0:T(4,128)S(1)} %add.15), channel_id=1, source_target_pairs={{0,2},{1,3},{2,0},{3,1},{4,6},{5,7},{6,4},{7,5},{8,10},{9,11},{10,... | collective-permute-start | bytes 294920 | tf_op jit(solution)/shard_map/ppermute | solution.py:226
  27.2 4.1 %collective-permute-done.5 = f32[3,8192]{1,0:T(4,128)S(1)} collective-permute-done((f32[3,8192]{1,0:T(4,128)S(1)}, f32[3,8192]{1,0:T(4,128)S(1)}, u32[]{:S(2)}, u32[]{:S(2)}) %collective-permute-start.5) | collective-permute-done | bytes 98336 | tf_op jit(solution)/shard_map/ppermute | solution.py:226
  31.3 0.1 collective-permute-start.6
  31.4 1.3 %collective-permute-done.6 = f32[3,8192]{1,0:T(4,128)S(1)} collective-permute-done((f32[3,8192]{1,0:T(4,128)S(1)}, f32[3,8192]{1,0:T(4,128)S(1)}, u32[]{:S(2)}, u32[]{:S(2)}) %collective-permute-start.6) | collective-permute-done | bytes 98336 | tf_op jit(solution)/shard_map/ppermute | solution.py:226
  32.7 0.8 %maximum_select_fusion = f32[3,16384]{1,0:T(4,128)} fusion(f32[3,8192]{1,0:T(4,128)S(1)} %collective-permute-done.6, f32[3,8192]{1,0:T(4,128)S(1)} %add.16, pred[]{:T(512)S(6)} %eq.5), kind=kLoop, calls=%fused_computation | loop fusion | flops 147456 | bytes 393217 | tf_op jit(solution)/shard_map/jit(_where)/select_n | solution.py:304
  (10 shorter events, 0.1 us)
Async XLA Ops:
  0.0 20.9 %copy-start = (f32[3,16384]{1,0:T(4,128)S(1)}, f32[3,16384]{1,0:T(4,128)}, u32[]{:S(2)}) copy-start(f32[3,16384]{1,0:T(4,128)} %refs_5_.1) | copy-start | bytes 589828
  0.0 20.9 %copy-start.1 = (f32[3,128,128]{2,1,0:T(8,128)S(1)}, f32[3,128,128]{2,1,0:T(8,128)}, u32[]{:S(2)}) copy-start(f32[3,128,128]{2,1,0:T(8,128)} %refs_9_.1) | copy-start | bytes 589828
  4.7 5.3 %collective-permute-start = (f32[136,128]{1,0:T(8,128)S(1)}, f32[136,128]{1,0:T(8,128)S(1)}, u32[]{:S(2)}, u32[]{:S(2)}) collective-permute-start(f32[136,128]{1,0:T(8,128)S(1)} %get-tuple-element.9), channel_id=1, source_target_pairs={{0,4},{4,0},{8,12},{12,8},{16,20},{20,16},{24,28},{28,24},{1,5},{5... | collective-permute-start | bytes 208904 | tf_op jit(solution)/shard_map/ppermute | solution.py:226
  10.1 10.9 %copy-start.3 = (s32[1,256]{1,0:T(1,128)S(1)}, s32[1,256]{1,0:T(1,128)}, u32[]{:S(2)}) copy-start(s32[1,256]{1,0:T(1,128)} %refs_7_.1) | copy-start | bytes 3076
  10.1 10.9 %copy-start.4 = (s32[1,256]{1,0:T(1,128)S(1)}, s32[1,256]{1,0:T(1,128)}, u32[]{:S(2)}) copy-start(s32[1,256]{1,0:T(1,128)} %refs_8_.1) | copy-start | bytes 3076
  10.1 10.9 %copy-start.5 = (f32[3,128]{1,0:T(4,128)S(1)}, f32[3,128]{1,0:T(4,128)}, u32[]{:S(2)}) copy-start(f32[3,128]{1,0:T(4,128)} %refs_10_.1) | copy-start | bytes 4612
  10.1 10.9 %copy-start.6 = (f32[3,128]{1,0:T(4,128)S(1)}, f32[3,128]{1,0:T(4,128)}, u32[]{:S(2)}) copy-start(f32[3,128]{1,0:T(4,128)} %refs_11_.1) | copy-start | bytes 4612
  10.1 10.9 %copy-start.2 = (f32[1,3,128]{2,0,1:T(1,128)S(1)}, f32[1,3,128]{2,0,1:T(1,128)}, u32[]{:S(2)}) copy-start(f32[1,3,128]{2,0,1:T(1,128)} %param.12) | copy-start | bytes 4612
  10.1 5.1 %collective-permute-start.1 = (f32[136,128]{1,0:T(8,128)S(1)}, f32[136,128]{1,0:T(8,128)S(1)}, u32[]{:S(2)}, u32[]{:S(2)}) collective-permute-start(f32[136,128]{1,0:T(8,128)S(1)} %add.14.refs_0_), channel_id=1, source_target_pairs={{0,8},{4,12},{8,0},{12,4},{16,24},{20,28},{24,16},{28,20},{1,9},{5... | collective-permute-start | bytes 208904 | tf_op jit(solution)/shard_map/ppermute | solution.py:226
  12.3 6.7 %collective-permute-start.2 = (f32[136,128]{1,0:T(8,128)S(1)}, f32[136,128]{1,0:T(8,128)S(1)}, u32[]{:S(2)}, u32[]{:S(2)}) collective-permute-start(f32[136,128]{1,0:T(8,128)S(1)} %add.14.refs_0_), channel_id=1, source_target_pairs={{0,16},{4,20},{8,24},{12,28},{16,0},{20,4},{24,8},{28,12},{1,17},{... | collective-permute-start | bytes 208904 | tf_op jit(solution)/shard_map/ppermute | solution.py:226
  14.8 6.1 %collective-permute-start.3 = (f32[136,128]{1,0:T(8,128)S(1)}, f32[136,128]{1,0:T(8,128)S(1)}, u32[]{:S(2)}, u32[]{:S(2)}) collective-permute-start(f32[136,128]{1,0:T(8,128)S(1)} %add.14.refs_0_), channel_id=1, source_target_pairs={{0,24},{4,28},{8,16},{12,20},{16,8},{20,12},{24,0},{28,4},{1,25},{... | collective-permute-start | bytes 208904 | tf_op jit(solution)/shard_map/ppermute | solution.py:226
  24.2 1.4 %collective-permute-start.4 = (f32[3,8192]{1,0:T(4,128)S(1)}, f32[3,8192]{1,0:T(4,128)S(1)}, u32[]{:S(2)}, u32[]{:S(2)}) collective-permute-start(f32[3,8192]{1,0:T(4,128)S(1)} %get-tuple-element.12), channel_id=1, source_target_pairs={{0,1},{1,0},{2,3},{3,2},{4,5},{5,4},{6,7},{7,6},{8,9},{9,8},{10,11... | collective-permute-start | bytes 294920 | tf_op jit(solution)/shard_map/ppermute | solution.py:226
  25.7 5.6 %collective-permute-start.5 = (f32[3,8192]{1,0:T(4,128)S(1)}, f32[3,8192]{1,0:T(4,128)S(1)}, u32[]{:S(2)}, u32[]{:S(2)}) collective-permute-start(f32[3,8192]{1,0:T(4,128)S(1)} %add.15), channel_id=1, source_target_pairs={{0,2},{1,3},{2,0},{3,1},{4,6},{5,7},{6,4},{7,5},{8,10},{9,11},{10,... | collective-permute-start | bytes 294920 | tf_op jit(solution)/shard_map/ppermute | solution.py:226
  31.3 1.4 %collective-permute-start.6 = (f32[3,8192]{1,0:T(4,128)S(1)}, f32[3,8192]{1,0:T(4,128)S(1)}, u32[]{:S(2)}, u32[]{:S(2)}) collective-permute-start(f32[3,8192]{1,0:T(4,128)S(1)} %add.16), channel_id=1, source_target_pairs={{0,1},{1,0},{2,3},{3,2},{4,5},{5,4},{6,7},{7,6},{8,9},{9,8},{10,11... | collective-permute-start | bytes 294920 | tf_op jit(solution)/shard_map/ppermute | solution.py:226

commit v3 on v2

--- a/solution.py
+++ b/solution.py
@@ -38,7 +38,17 @@
 
 
 def lane_gather(table, index):
-    return jnp.take_along_axis(table, index, axis=1, mode="promise_in_bounds")
+    numbers = lax.GatherDimensionNumbers(
+        offset_dims=(),
+        collapsed_slice_dims=(1,),
+        start_index_map=(1,),
+        operand_batching_dims=(0,),
+        start_indices_batching_dims=(0,),
+    )
+    return lax.gather(
+        table, index[..., None], numbers, (1, 1),
+        mode=lax.GatherScatterMode.PROMISE_IN_BOUNDS,
+    )
 
 
 def pair_centres(cen_ref, halo_row):
@@ -156,18 +166,42 @@
         out_ref[halos + at : halos + at + 1, :] = phi[:, at * LANES : (at + 1) * LANES]
 
 
-def relax_kernel(count, halo_axis, *refs):
-    profile_refs = refs[:count]
-    (
-        u_ref, pos_ref, cen_ref, halo_ref, tile_ref, mix_ref, drive_ref, readout_ref,
-        keep_ref, send_ref, state_ref, base_ref, weight_ref, table_ref, sum_ref,
-    ) = refs[count:]
+def prepare_kernel(
+    halo_axis, u_ref, cen_ref, halo_ref, tile_ref, mix_ref, drive_ref, readout_ref,
+    weight_ref, owner_ref, left_ref, index_ref, part_ref, gains_ref,
+):
     pairs, halos = halo_ref.shape[1], cen_ref.shape[2]
-    tiles, knots = pos_ref.shape[1] // BLK, drive_ref.shape[1]
+    tiles = left_ref.shape[0] // 8
     for comp in range(3):
         high, low = parts_of(mix_ref[comp], 2)
         both = jnp.concatenate([high, low], axis=1)
         weight_ref[comp] = jnp.concatenate([both, both], axis=0)
+    halo_row = halo_ref[...]
+    halo_column = jnp.transpose(jnp.broadcast_to(halo_row, (8, pairs)).astype(F32))[:, :1]
+    owner = halo_column.astype(jnp.int32) == iota((pairs, halos), 1)
+    owner_ref[...] = jnp.where(owner, 1.0, 0.0).astype(BF16)
+    high, low = [part.astype(F32) for part in parts_of(pair_centres(cen_ref, halo_row), 2)]
+    kinds = jnp.concatenate([high[:3], jnp.ones((1, pairs), F32), low[:4]], axis=0)
+    first = (lax.axis_index(halo_axis) & 1) * (tiles // 2)
+    tile_row = jnp.broadcast_to(tile_ref[...], (8, pairs)) ^ first
+    left = jnp.concatenate([jnp.where(tile_row == at, kinds, 0.0) for at in range(tiles)], axis=0)
+    left_ref[...] = left.astype(BF16)
+    index = u_ref[...].astype(jnp.int32)
+    index_ref[...] = index
+    part_ref[...] = u_ref[...] - index.astype(F32)
+    gains_ref[:3, :] = drive_ref[...]
+    gains_ref[3:6, :] = readout_ref[...]
+    gains_ref[6:, :] = jnp.zeros_like(gains_ref[6:, :])
+
+
+def relax_kernel(count, halo_axis, *refs):
+    profile_refs = refs[:count]
+    (
+        weight_ref, owner_ref, left_ref, index_ref, part_ref, gains_ref, pos_ref,
+        keep_ref, send_ref, state_ref, base_ref, table_ref,
+    ) = refs[count:]
+    halos = owner_ref.shape[1]
+    tiles, knots = pos_ref.shape[1] // BLK, gains_ref.shape[1]
     extra = sum(ref[halos:, :] for ref in profile_refs)
     phi_columns = jnp.transpose(extra)
     for block in range(halos // LANES):
@@ -175,7 +209,7 @@
         level = jnp.log1p(sum(ref[rows, :] for ref in profile_refs))
         phi = phi_columns[:, block : block + 1]
         for comp in range(3):
-            base = drive_ref[comp : comp + 1, :] * level
+            base = gains_ref[comp : comp + 1, :] * level
             base_ref[comp] = base
             state_ref[comp] = jnp.tanh(base)
 
@@ -189,37 +223,36 @@
                 state_ref[comp] = jnp.tanh(base_ref[comp] + phi * mixed + half_mean)
             return carry
 
-        lax.fori_loop(0, ITERS - 1, step, 0)
-        coef = sum(state_ref[comp] * readout_ref[comp : comp + 1, :] for comp in range(3))
+        lax.fori_loop(0, ITERS - 1, step, 0, unroll=True)
+        coef = sum(state_ref[comp] * gains_ref[3 + comp : 4 + comp, :] for comp in range(3))
         table_ref[rows, :knots] = coef
         table_ref[rows, knots:] = pltpu.roll(coef, knots - 1, 1) - coef
 
-    halo_row, tile_row = halo_ref[...], tile_ref[...]
-    halo_column = jnp.transpose(jnp.broadcast_to(halo_row, (8, pairs)).astype(F32))[:, :1]
-    owner = jnp.where(halo_column.astype(jnp.int32) == iota((pairs, halos), 1), 1.0, 0.0).astype(BF16)
-    tables = sum(bdot(owner, part) for part in parts_of(table_ref[...], 2))
-    centre = pair_centres(cen_ref, halo_row)
-    high, low = [part.astype(F32) for part in parts_of(centre, 2)]
-    kinds = jnp.concatenate([high[:3], jnp.ones((1, pairs), F32), low[:4]], axis=0)
-    tile_row = jnp.broadcast_to(tile_row, (8, pairs))
-    left = jnp.concatenate([jnp.where(tile_row == at, kinds, 0.0) for at in range(tiles)], axis=0)
-    left = left.astype(BF16)
-    for at in range(BLK // LANES):
-        u = u_ref[:, at * LANES : (at + 1) * LANES]
-        whole = jnp.floor(u)
-        index = whole.astype(jnp.int32)
-        start = lane_gather(tables[:, :knots], index)
-        slope = lane_gather(tables[:, knots:], index)
-        high, low = parts_of(start + (u - whole) * slope, 2)
-        sum_ref[:, at * LANES : (at + 1) * LANES] = bdot(left, high) + bdot(left, low)
+    owner = owner_ref[...]
+    tables = bdot(
+        jnp.concatenate([owner] * 2, axis=1), jnp.concatenate(parts_of(table_ref[...], 2), axis=0)
+    )
+    left = left_ref[...]
+    left = jnp.concatenate([left] * 2, axis=1)
     half = tiles // 2
-    bit = lax.axis_index(halo_axis) & 1
-    for ref, which in ((keep_ref, bit), (send_ref, 1 - bit)):
-        for at in range(half):
-            tile = which * half + at
-            rows = sum_ref[pl.ds(pl.multiple_of(tile * 8, 8), 8), :]
-            pos = pos_ref[:, pl.ds(pl.multiple_of(tile * BLK, BLK), BLK)]
-            ref[:, at * BLK : (at + 1) * BLK] = pos * rows[3:4] - rows[:3] - rows[4:7]
+    first = (lax.axis_index(halo_axis) & 1) * half
+    width = 2 * LANES
+    for at in range(0, BLK, width):
+        scalars = []
+        for lanes in (slice(at, at + LANES), slice(at + LANES, at + width)):
+            index = index_ref[:, lanes]
+            start = lane_gather(tables[:, :knots], index)
+            slope = lane_gather(tables[:, knots:], index)
+            scalars.append(start + part_ref[:, lanes] * slope)
+        sums = bdot(left, jnp.concatenate(parts_of(jnp.concatenate(scalars, axis=1), 2), axis=0))
+        for ref, start in ((keep_ref, 0), (send_ref, half)):
+            for tile in range(half):
+                rows = sums[8 * (start + tile) : 8 * (start + tile + 1)]
+                lane = pl.multiple_of(((start + tile) ^ first) * BLK + at, width)
+                pos = pos_ref[:, pl.ds(lane, width)]
+                ref[:, tile * BLK + at : tile * BLK + at + width] = (
+                    pos * rows[3:4] - rows[:3] - rows[4:7]
+                )
 
 
 def butterfly(value, name, size, distance):
@@ -274,26 +307,36 @@
     held, distance = [profile], 1
     while distance < n_space:
         total = sum(held[1:], held[0])
-        if distance == 1 or distance * 2 == n_space:
-            steps = [distance]
-        else:
-            steps = [distance, 2 * distance, 3 * distance]
-        held = [total] + [butterfly(total, "space", n_space, step) for step in steps]
-        distance *= 2 * len(steps) if len(steps) == 1 else 4
+        steps = [3, 2, 1] if 4 * distance <= n_space else [1]
+        held = [total] + [butterfly(total, "space", n_space, step * distance) for step in steps]
+        distance *= len(steps) + 1
+    weight, owner, left, index, part, gains = pl.pallas_call(
+        functools.partial(prepare_kernel, "halo"),
+        out_shape=(
+            jax.ShapeDtypeStruct((3, 2 * knots, 2 * knots), BF16),
+            jax.ShapeDtypeStruct((pairs, halos), BF16),
+            jax.ShapeDtypeStruct((8 * tiles, pairs), BF16),
+            jax.ShapeDtypeStruct((pairs, BLK), jnp.int32),
+            jax.ShapeDtypeStruct((pairs, BLK), F32),
+            jax.ShapeDtypeStruct((8, knots), F32),
+        ),
+        in_specs=[vmem] * 7,
+        out_specs=(vmem,) * 6,
+        compiler_params=room,
+        cost_estimate=pl.CostEstimate(flops=0, bytes_accessed=4 << 20, transcendentals=0),
+    )(u, centres, pair_halo, pair_tile, mixing, drive, readout)
     keep, send = pl.pallas_call(
         functools.partial(relax_kernel, len(held), "halo"),
         out_shape=(jax.ShapeDtypeStruct((3, particles // 2), F32),) * 2,
-        in_specs=[vmem] * (len(held) + 8),
+        in_specs=[vmem] * (len(held) + 7),
         out_specs=(vmem,) * 2,
         scratch_shapes=[
             pltpu.VMEM((3, LANES, knots), F32),
             pltpu.VMEM((3, LANES, knots), F32),
-            pltpu.VMEM((3, 2 * knots, 2 * knots), BF16),
             pltpu.VMEM((halos, 2 * knots), F32),
-            pltpu.VMEM((8 * tiles, BLK), F32),
         ],
         compiler_params=room,
-    )(*held, u, positions, centres, pair_halo, pair_tile, mixing, drive, readout)
+    )(*held, weight, owner, left, index, part, gains, positions)
     keep = keep + butterfly(send, "halo", n_halo, 1)
     distance = 2
     while distance < n_halo:

time: 33.6 us -> 30.6 us (0.911)
  waiting for transfers between devices: 15.1 us -> 13.1 us
  Pallas kernels: 7.92 us -> 7.31 us
  starting transfers between devices: 9.49 us -> 9.07 us
    ppermute x7, waiting for transfers between devices: 15.1 us -> 13.1 us  [butterfly(): lax.ppermute(value, name, [(at, at ^ distance) for at in range(size)])]
    pallas_call x1, Pallas kernels: 3.21 us -> 2.34 us  [per_device(): pl.pallas_call(functools.partial(relax_kernel, len(held), 'halo'), out_sh...]
    ppermute x7, starting transfers between devices: 9.49 us -> 9.07 us  [butterfly(): lax.ppermute(value, name, [(at, at ^ distance) for at in range(size)])]
  transfers between devices with their start and end apart: 7 -> 7, of which waited for: 7 -> 7; matrix products, arithmetic and copies ran while one was open for 0% -> 0% of each run, Pallas kernels for 0% -> 1%
where the time goes in v3:
time: 30.6 us; the launch traced here: 30.5 us
  waiting for transfers between devices  13.1 us (43%)
  starting transfers between devices  9.07 us (30%)
  Pallas kernels  7.31 us (24%)
  other arithmetic  0.86 us (3%)
    ppermute x7, waiting for transfers between devices, butterfly(): lax.ppermute(value, name, [(at, at ^ distance) for at in range(size)])  13.1 us
    ppermute x7, starting transfers between devices, butterfly(): lax.ppermute(value, name, [(at, at ^ distance) for at in range(size)])  9.07 us
    pallas_call x1, Pallas kernels, per_device(): pl.pallas_call(project_kernel, out_shape=(jax.ShapeDtypeStruct((rows, kno...  4.65 us
    pallas_call x1, Pallas kernels, per_device(): pl.pallas_call(functools.partial(relax_kernel, len(held), 'halo'), out_sh...  2.34 us
    select_n x1, other arithmetic, per_device(): jnp.where(first, jnp.concatenate([keep, other], axis=1), jnp.concatenate(...  0.76 us
  transfers between devices with their start and end apart: 7, of which 7 were waited for; matrix products, arithmetic and copies ran while one was open for 0% of the time, Pallas kernels for 1%

profile of v3, /device:TPU:0, one launch (start us, length us, event | category | flops | bytes accessed | tf_op | source)
XLA Modules:
  0.0 30.5 jit_solution(10197938832486227348)
XLA Ops:
  0.0 4.7 %shard_map.100 = (f32[136,128]{1,0:T(8,128)S(1)}, f32[256,512]{1,0:T(8,128)S(1)}) custom-call(f32[3,16384]{1,0:T(4,128)} %refs_8_.1, f32[128,128]{1,0:T(8,128)} %bitcast.4, f32[3,1,128]{2,1,0:T(1,128)} %bitcast.2, s32[1,256]{1,0:T(1,128)} %halo_ref.1, s32[1,256]{1,0:T(1,128)} %tile_ref.1, s32[1,128]{1,0:T(1,128)} %slot_hbm.1, f32[1,16]{1,0:T(1,128)} %feed_hbm.1), custom_call_target="tpu_custom_call" | custom-call | tf_op jit(solution)/shard_map/pallas_call | solution.py:276
  4.7 0.0 copy-start.1
  4.7 4.1 %collective-permute-start = (f32[136,128]{1,0:T(8,128)S(1)}, f32[136,128]{1,0:T(8,128)S(1)}, u32[]{:S(2)}, u32[]{:S(2)}) collective-permute-start(f32[136,128]{1,0:T(8,128)S(1)} %get-tuple-element.15), channel_id=1, source_target_pairs={{0,12},{4,8},{8,4},{12,0},{16,28},{20,24},{24,20},{28,16},{1,13},{... | collective-permute-start | bytes 208904 | tf_op jit(solution)/shard_map/ppermute | solution.py:259
  8.7 0.5 %collective-permute-start.1 = (f32[136,128]{1,0:T(8,128)S(1)}, f32[136,128]{1,0:T(8,128)S(1)}, u32[]{:S(2)}, u32[]{:S(2)}) collective-permute-start(f32[136,128]{1,0:T(8,128)S(1)} %get-tuple-element.15), channel_id=1, source_target_pairs={{0,8},{4,12},{8,0},{12,4},{16,24},{20,28},{24,16},{28,20},{1,9},{5... | collective-permute-start | bytes 208904 | tf_op jit(solution)/shard_map/ppermute | solution.py:259
  9.2 0.2 collective-permute-start.2
  9.4 1.8 %collective-permute-done = f32[136,128]{1,0:T(8,128)S(1)} collective-permute-done((f32[136,128]{1,0:T(8,128)S(1)}, f32[136,128]{1,0:T(8,128)S(1)}, u32[]{:S(2)}, u32[]{:S(2)}) %collective-permute-start) | collective-permute-done | bytes 69664 | tf_op jit(solution)/shard_map/ppermute | solution.py:259
  11.2 1.8 %collective-permute-done.1 = f32[136,128]{1,0:T(8,128)S(1)} collective-permute-done((f32[136,128]{1,0:T(8,128)S(1)}, f32[136,128]{1,0:T(8,128)S(1)}, u32[]{:S(2)}, u32[]{:S(2)}) %collective-permute-start.1) | collective-permute-done | bytes 69664 | tf_op jit(solution)/shard_map/ppermute | solution.py:259
  13.1 0.5 %collective-permute-done.2 = f32[136,128]{1,0:T(8,128)S(1)} collective-permute-done((f32[136,128]{1,0:T(8,128)S(1)}, f32[136,128]{1,0:T(8,128)S(1)}, u32[]{:S(2)}, u32[]{:S(2)}) %collective-permute-start.2) | collective-permute-done | bytes 69664 | tf_op jit(solution)/shard_map/ppermute | solution.py:259
  13.6 2.7 %collective-permute-start.3 = (f32[136,128]{1,0:T(8,128)S(1)}, f32[136,128]{1,0:T(8,128)S(1)}, u32[]{:S(2)}, u32[]{:S(2)}) collective-permute-start(f32[136,128]{1,0:T(8,128)S(1)} %add_add_fusion.refs_0_), channel_id=1, source_target_pairs={{0,16},{4,20},{8,24},{12,28},{16,0},{20,4},{24,8},{28,12},{1,17},{... | collective-permute-start | bytes 208904 | tf_op jit(solution)/shard_map/ppermute | solution.py:259
  16.2 0.0 copy-done.1
  16.2 0.0 copy-done.3
  16.2 0.0 copy-done.4
  16.2 0.0 copy-done.5
  16.2 0.0 copy-start
  16.3 0.3 %shard_map.101 = (bf16[3,256,256]{2,1,0:T(8,128)(2,1)S(1)}, bf16[256,128]{1,0:T(8,128)(2,1)S(1)}, bf16[256,256]{1,0:T(8,128)(2,1)S(1)}, s32[256,512]{1,0:T(8,128...) custom-call(f32[256,512]{1,0:T(8,128)S(1)} %get-tuple-element.16.u_ref, f32[3,1,128]{2,1,0:T(1,128)S(1)} %bitcast.3, ...), custom_call_target="tpu_custom_call" | custom-call | bytes 4194304 | tf_op jit(solution)/shard_map/pallas_call | solution.py:313
  16.6 2.2 %collective-permute-done.3.refs_1_ = f32[136,128]{1,0:T(8,128)S(1)} collective-permute-done((f32[136,128]{1,0:T(8,128)S(1)}, f32[136,128]{1,0:T(8,128)S(1)}, u32[]{:S(2)}, u32[]{:S(2)}) %collective-permute-start.3) | collective-permute-done | bytes 69664 | tf_op jit(solution)/shard_map/ppermute | solution.py:259
  18.8 2.3 %shard_map.102 = (f32[3,8192]{1,0:T(4,128)S(1)}, f32[3,8192]{1,0:T(4,128)S(1)}) custom-call(f32[136,128]{1,0:T(8,128)S(1)} %add_add_fusion.refs_0_, f32[136,128]{1,0:T(8,128)S(1)} %collective-permute-done.3.refs_1_, bf16[3,256,256]{2,1,0:T(8,128)(2,1)S(1)} %get-tuple-element.17.refs_2_, bf16[256,128]{1,0:T(8,128)(2,1)S(1)} %get-tuple-element.18.refs_3_, ...), custom_call_target="tpu_custom_call" | custom-call | tf_op jit(solution)/shard_map/pallas_call | solution.py:328
  21.2 0.1 collective-permute-start.4
  21.3 1.3 %collective-permute-done.4 = f32[3,8192]{1,0:T(4,128)S(1)} collective-permute-done((f32[3,8192]{1,0:T(4,128)S(1)}, f32[3,8192]{1,0:T(4,128)S(1)}, u32[]{:S(2)}, u32[]{:S(2)}) %collective-permute-start.4) | collective-permute-done | bytes 98336 | tf_op jit(solution)/shard_map/ppermute | solution.py:259
  22.6 1.6 %collective-permute-start.5 = (f32[3,8192]{1,0:T(4,128)S(1)}, f32[3,8192]{1,0:T(4,128)S(1)}, u32[]{:S(2)}, u32[]{:S(2)}) collective-permute-start(f32[3,8192]{1,0:T(4,128)S(1)} %add.23), channel_id=1, source_target_pairs={{0,2},{1,3},{2,0},{3,1},{4,6},{5,7},{6,4},{7,5},{8,10},{9,11},{10,... | collective-permute-start | bytes 294920 | tf_op jit(solution)/shard_map/ppermute | solution.py:259
  24.2 4.1 %collective-permute-done.5 = f32[3,8192]{1,0:T(4,128)S(1)} collective-permute-done((f32[3,8192]{1,0:T(4,128)S(1)}, f32[3,8192]{1,0:T(4,128)S(1)}, u32[]{:S(2)}, u32[]{:S(2)}) %collective-permute-start.5) | collective-permute-done | bytes 98336 | tf_op jit(solution)/shard_map/ppermute | solution.py:259
  28.3 0.1 collective-permute-start.6
  28.4 1.3 %collective-permute-done.6 = f32[3,8192]{1,0:T(4,128)S(1)} collective-permute-done((f32[3,8192]{1,0:T(4,128)S(1)}, f32[3,8192]{1,0:T(4,128)S(1)}, u32[]{:S(2)}, u32[]{:S(2)}) %collective-permute-start.6) | collective-permute-done | bytes 98336 | tf_op jit(solution)/shard_map/ppermute | solution.py:259
  29.7 0.8 %maximum_select_fusion = f32[3,16384]{1,0:T(4,128)} fusion(f32[3,8192]{1,0:T(4,128)S(1)} %collective-permute-done.6, f32[3,8192]{1,0:T(4,128)S(1)} %add.24, pred[]{:T(512)S(6)} %eq.5), kind=kLoop, calls=%fused_computation | loop fusion | flops 147456 | bytes 393217 | tf_op jit(solution)/shard_map/jit(_where)/select_n | solution.py:347
  (11 shorter events, 0.1 us)
Async XLA Ops:
  4.7 11.6 %copy-start.1 = (f32[3,128,128]{2,1,0:T(8,128)S(1)}, f32[3,128,128]{2,1,0:T(8,128)}, u32[]{:S(2)}) copy-start(f32[3,128,128]{2,1,0:T(8,128)} %mix_ref.1) | copy-start | bytes 589828
  4.7 6.6 %collective-permute-start = (f32[136,128]{1,0:T(8,128)S(1)}, f32[136,128]{1,0:T(8,128)S(1)}, u32[]{:S(2)}, u32[]{:S(2)}) collective-permute-start(f32[136,128]{1,0:T(8,128)S(1)} %get-tuple-element.15), channel_id=1, source_target_pairs={{0,12},{4,8},{8,4},{12,0},{16,28},{20,24},{24,20},{28,16},{1,13},{... | collective-permute-start | bytes 208904 | tf_op jit(solution)/shard_map/ppermute | solution.py:259
  8.7 4.3 %collective-permute-start.1 = (f32[136,128]{1,0:T(8,128)S(1)}, f32[136,128]{1,0:T(8,128)S(1)}, u32[]{:S(2)}, u32[]{:S(2)}) collective-permute-start(f32[136,128]{1,0:T(8,128)S(1)} %get-tuple-element.15), channel_id=1, source_target_pairs={{0,8},{4,12},{8,0},{12,4},{16,24},{20,28},{24,16},{28,20},{1,9},{5... | collective-permute-start | bytes 208904 | tf_op jit(solution)/shard_map/ppermute | solution.py:259
  9.2 4.3 %collective-permute-start.2 = (f32[136,128]{1,0:T(8,128)S(1)}, f32[136,128]{1,0:T(8,128)S(1)}, u32[]{:S(2)}, u32[]{:S(2)}) collective-permute-start(f32[136,128]{1,0:T(8,128)S(1)} %get-tuple-element.15), channel_id=1, source_target_pairs={{0,4},{4,0},{8,12},{12,8},{16,20},{20,16},{24,28},{28,24},{1,5},{5... | collective-permute-start | bytes 208904 | tf_op jit(solution)/shard_map/ppermute | solution.py:259
  13.5 2.7 %copy-start.3 = (s32[1,256]{1,0:T(1,128)S(1)}, s32[1,256]{1,0:T(1,128)}, u32[]{:S(2)}) copy-start(s32[1,256]{1,0:T(1,128)} %halo_ref.1) | copy-start | bytes 3076
  13.5 2.7 %copy-start.4 = (s32[1,256]{1,0:T(1,128)S(1)}, s32[1,256]{1,0:T(1,128)}, u32[]{:S(2)}) copy-start(s32[1,256]{1,0:T(1,128)} %tile_ref.1) | copy-start | bytes 3076
  13.5 2.7 %copy-start.5 = (f32[3,128]{1,0:T(4,128)S(1)}, f32[3,128]{1,0:T(4,128)}, u32[]{:S(2)}) copy-start(f32[3,128]{1,0:T(4,128)} %drive_ref.1) | copy-start | bytes 4612
  13.5 2.7 %copy-start.6 = (f32[3,128]{1,0:T(4,128)S(1)}, f32[3,128]{1,0:T(4,128)}, u32[]{:S(2)}) copy-start(f32[3,128]{1,0:T(4,128)} %readout_ref.1) | copy-start | bytes 4612
  13.5 2.7 %copy-start.2 = (f32[1,3,128]{2,0,1:T(1,128)S(1)}, f32[1,3,128]{2,0,1:T(1,128)}, u32[]{:S(2)}) copy-start(f32[1,3,128]{2,0,1:T(1,128)} %param.12) | copy-start | bytes 4612
  13.6 5.3 %collective-permute-start.3 = (f32[136,128]{1,0:T(8,128)S(1)}, f32[136,128]{1,0:T(8,128)S(1)}, u32[]{:S(2)}, u32[]{:S(2)}) collective-permute-start(f32[136,128]{1,0:T(8,128)S(1)} %add_add_fusion.refs_0_), channel_id=1, source_target_pairs={{0,16},{4,20},{8,24},{12,28},{16,0},{20,4},{24,8},{28,12},{1,17},{... | collective-permute-start | bytes 208904 | tf_op jit(solution)/shard_map/ppermute | solution.py:259
  16.2 2.6 %copy-start = (f32[3,16384]{1,0:T(4,128)S(1)}, f32[3,16384]{1,0:T(4,128)}, u32[]{:S(2)}) copy-start(f32[3,16384]{1,0:T(4,128)} %refs_8_.1) | copy-start | bytes 589828
  21.2 1.4 %collective-permute-start.4 = (f32[3,8192]{1,0:T(4,128)S(1)}, f32[3,8192]{1,0:T(4,128)S(1)}, u32[]{:S(2)}, u32[]{:S(2)}) collective-permute-start(f32[3,8192]{1,0:T(4,128)S(1)} %get-tuple-element.24), channel_id=1, source_target_pairs={{0,1},{1,0},{2,3},{3,2},{4,5},{5,4},{6,7},{7,6},{8,9},{9,8},{10,11... | collective-permute-start | bytes 294920 | tf_op jit(solution)/shard_map/ppermute | solution.py:259
  22.6 5.6 %collective-permute-start.5 = (f32[3,8192]{1,0:T(4,128)S(1)}, f32[3,8192]{1,0:T(4,128)S(1)}, u32[]{:S(2)}, u32[]{:S(2)}) collective-permute-start(f32[3,8192]{1,0:T(4,128)S(1)} %add.23), channel_id=1, source_target_pairs={{0,2},{1,3},{2,0},{3,1},{4,6},{5,7},{6,4},{7,5},{8,10},{9,11},{10,... | collective-permute-start | bytes 294920 | tf_op jit(solution)/shard_map/ppermute | solution.py:259
  28.3 1.4 %collective-permute-start.6 = (f32[3,8192]{1,0:T(4,128)S(1)}, f32[3,8192]{1,0:T(4,128)S(1)}, u32[]{:S(2)}, u32[]{:S(2)}) collective-permute-start(f32[3,8192]{1,0:T(4,128)S(1)} %add.24), channel_id=1, source_target_pairs={{0,1},{1,0},{2,3},{3,2},{4,5},{5,4},{6,7},{7,6},{8,9},{9,8},{10,11... | collective-permute-start | bytes 294920 | tf_op jit(solution)/shard_map/ppermute | solution.py:259
